TPU v7x, 32 devices: a whole 2x2x4 slice. The times are simulated.
32 devices in a mesh: row: 8 (over z, core), col: 4 (over y, x).
Axes of the slice: x: 2, y: 2, z: 4, core: 2. Of those that a mesh axis runs over, the one named last changes fastest.
Arguments:
- diag_tile: float32 [128, 128], P('row'), may hold values from -20 to 100, as said below
- panel: bfloat16 [16384, 128], P(('row', 'col')), may hold values from -1.796875 to 1.796875
- trailing: float32 [16384, 2048], P('row', 'col'), may hold values from -6 to 6
Outputs:
- solved: bfloat16 [16384, 128], P(('row', 'col'))
- updated: float32 [16384, 2048], P('row', 'col')
Inputs may be any that keep to these rules, and one draw needn't show every extreme that they name: diag_tile is symmetric and positive definite, with its smallest eigenvalue 1 or more.
All inputs are finite; a program needn't handle non-finite values.
Results may differ from a plain program's by a relative error of at most 0.0051.
Values may be sent and summed in bfloat16 or wider, within the bound.
No kernel may reach another device: no remote copies, remote signals or barrier semaphores. Data moves between devices by JAX's collectives and lax.ppermute only.
A program may use at most 64 MiB of HBM per device.

v0:
```python
import jax
import jax.numpy as jnp
from jax import lax
from jax.sharding import PartitionSpec as P


def from_root(value, axis, source):
    kept = jnp.where(lax.axis_index(axis) == source, value, 0).astype(value.dtype)
    return lax.psum(kept, axis)


def per_device(diag_tile, panel, trailing):
    whole_tile = lax.all_gather(diag_tile, "row", axis=0, tiled=True)
    factor = jnp.linalg.cholesky(whole_tile)
    identity = jnp.eye(whole_tile.shape[0], dtype=whole_tile.dtype)
    inverse = lax.linalg.triangular_solve(factor, identity, left_side=True, lower=True).astype(
        jnp.bfloat16
    )
    solved_rows = lax.dot_general(
        panel, inverse, (((1,), (1,)), ((), ())), preferred_element_type=jnp.float32
    ).astype(jnp.bfloat16)
    row_panel = lax.all_gather(solved_rows, "col", axis=0, tiled=True)
    rows_dev = row_panel.shape[0]
    cols_dev = trailing.shape[1]
    col_start = lax.axis_index("col") * cols_dev
    source_row = col_start // rows_dev
    offset = col_start % rows_dev
    picked = lax.dynamic_slice_in_dim(row_panel, offset, cols_dev, 0)
    col_panel = from_root(picked, "row", source_row)
    update = lax.dot_general(
        row_panel, col_panel, (((1,), (1,)), ((), ())), preferred_element_type=jnp.float32
    )
    row_ids = lax.axis_index("row") * rows_dev + jnp.arange(rows_dev, dtype=jnp.int32)
    col_ids = col_start + jnp.arange(cols_dev, dtype=jnp.int32)
    lower_part = row_ids[:, None] >= col_ids[None, :]
    updated = jnp.where(lower_part, trailing - update, trailing)
    return (solved_rows, updated)


def solution(mesh):
    in_specs = (P("row", None), P(("row", "col"), None), P("row", "col"))
    out_specs = (P(("row", "col"), None), P("row", "col"))
    return jax.shard_map(
        per_device, mesh=mesh, in_specs=in_specs, out_specs=out_specs, check_vma=False
    )
```

profile of v0, /device:TPU:0, one launch (start us, length us, event | category | flops | bytes accessed | tf_op | source)
XLA Modules:
  0.0 123.7 jit_solution(9039450617726350077)
XLA Ops:
  7.2 0.0 copy-start
  7.2 0.0 all-reduce.2.cloned.1.call-start
  7.2 15.9 %all_gather.6 = f32[128,128]{1,0:T(8,128)S(1)} all-gather(f32[16,128]{1,0:T(8,128)} %param.3), channel_id=1, replica_groups=mesh['row'=8,'col'=4] {'row'}, dimensions={0}, use_global_device_ids=true | all-gather | bytes 73728 | tf_op jit(solution)/shard_map/all_gather | solution.py:13
  23.2 0.1 copy.8
  23.3 11.7 %cholesky.17 = f32[128,128]{1,0:T(8,128)S(1)} custom-call(f32[128,128]{1,0:T(8,128)S(1)} %fusion.3), custom_call_target="Cholesky" | custom-call | tf_op jit(solution)/shard_map/jit(cholesky)/cholesky | solution.py:14
  35.0 0.6 compare_reduce_fusion
  35.7 0.7 fusion.1
  36.3 9.8 %custom-call.6 = f32[1,128,128]{1,2,0:T(8,128)S(1)} custom-call(f32[1,128,128]{2,1,0:T(8,128)S(1)} %fusion.1), custom_call_target="InvertDiagBlocksLowerTriangular" | custom-call | tf_op jit(solution)/shard_map/triangular_solve | solution.py:16
  46.1 0.3 convolution_convert_fusion.1
  46.4 0.0 copy-done
  46.4 0.2 fusion
  46.6 10.3 %all_gather.7 = bf16[2048,128]{0,1:T(8,128)(2,1)S(1)} all-gather(bf16[512,128]{0,1:T(8,128)(2,1)S(1)} %fusion), channel_id=1, replica_groups=mesh['row'=8,'col'=4] {'col'}, dimensions={0}, use_global_device_ids=true | all-gather | bytes 655360 | tf_op jit(solution)/shard_map/all_gather | solution.py:22
  56.9 0.7 dynamic-slice_select_fusion
  57.6 0.0 all-reduce.2.cloned.1.call-update
  57.6 0.8 copy.9
  58.4 54.4 %all-reduce.2.cloned.1.call-done = bf16[512,128]{0,1:T(8,128)(2,1)} async-done(((bf16[512,128]{0,1:T(8,128)(2,1)}), bf16[512,128]{0,1:T(8,128)(2,1)}) %all-reduce.2.cloned.1.call-update) | async-done | bytes 131088 | tf_op jit(solution)/shard_map/psum | solution.py:9
  112.8 4.1 %subtract_select_fusion = f32[2048,512]{1,0:T(8,128)} fusion(f32[2048,512]{1,0:T(8,128)} %param.5, bf16[2048,128]{0,1:T(8,128)(2,1)S(1)} %all_gather.7, bf16[512,128]{0,1:T(8,128)(2,1)} %all-reduce.2.cloned.1.call-done, s32[512]{0:T(512)S(1)} %iota_add_fusion.1, s32[2048]{0:T(1024)S(1)} %iota_add_fusion), kind=kOutput, calls=%fused_computation | convolution fusion | flops 271581184 | bytes 9054208 | tf_op jit(solution)/shard_map/dot_general | solution.py:30
  (4 shorter events, 0.1 us)
Async XLA Ops:
  7.2 39.2 %copy-start = (bf16[512,128]{1,0:T(8,128)(2,1)S(1)}, bf16[512,128]{1,0:T(8,128)(2,1)}, u32[]{:S(2)}) copy-start(bf16[512,128]{1,0:T(8,128)(2,1)} %param.4) | copy-start | bytes 393220
  7.2 105.6 %all-reduce.2.cloned.1.call-start = ((), (), s32[]{:S(2)}) async-start(), calls=%async_computation | async-start | bytes 262144 | tf_op jit(solution)/shard_map/psum | solution.py:9
Sparse Core Ops, SparseCore 0:
  57.7 55.0 all-reduce.1
where the time goes:
time: 124 us
  waiting for transfers between devices  54.4 us (44%)
  blocking collectives  26.2 us (21%)
  other arithmetic  23.6 us (19%)
  between operations  14.1 us (11%)
  matrix products  4.52 us (4%)
    psum x1, waiting for transfers between devices, from_root(): return lax.psum(kept, axis)  54.4 us
    all_gather x1, blocking collectives, per_device(): whole_tile = lax.all_gather(diag_tile, 'row', axis=0, tiled=True)  15.9 us
    another operation x3, other arithmetic, per_device(): factor = jnp.linalg.cholesky(whole_tile)  12.4 us
    another operation x2, other arithmetic, per_device(): lax.linalg.triangular_solve(factor, identity, left_side=True, lower=True)  10.5 us
    all_gather x1, blocking collectives, per_device(): row_panel = lax.all_gather(solved_rows, 'col', axis=0, tiled=True)  10.3 us
    dot_general x1, matrix products, per_device(): lax.dot_general(row_panel, col_panel, (((1,), (1,)), ((), ())), preferred...  4.08 us
  transfers between devices with their start and end apart: 1, of which 1 were waited for; matrix products, arithmetic and copies ran while one was open for 1% of the time, Pallas kernels for 0%

commit v1 on v0

v1 whole, which is shorter than its diff:
```python
import functools

import jax
import jax.numpy as jnp
from jax import lax
from jax.experimental import pallas as pl
from jax.experimental.pallas import tpu as pltpu
from jax.sharding import PartitionSpec as P


SUB = 8
CHUNK = 256

VMEM = pl.BlockSpec(memory_space=pltpu.VMEM)
HBM = pl.BlockSpec(memory_space=pltpu.HBM)


def exchange(value, axis, size, step):
    return lax.ppermute(value, axis, [(i, i ^ step) for i in range(size)])


def far_steps(n_row):
    return [2 * i for i in reversed(range(1, n_row // 2))]


def inverse_factor(tile):
    n = tile[0].shape[1]
    blocks = n // SUB
    rows = list(tile)
    lane = lax.broadcasted_iota(jnp.int32, (SUB, n), 1)
    sub = lax.broadcasted_iota(jnp.int32, (SUB, n), 0)

    def col(x, c):
        return jnp.broadcast_to(x[:, c : c + 1], (SUB, n))

    def row(x, r):
        return jnp.broadcast_to(x[r : r + 1, :], (SUB, n))

    out = []
    for block in range(blocks):
        base = block * SUB
        inside = (lane >= base) & (lane < base + SUB)
        here = rows[block]
        cols = [col(here, base + j) for j in range(SUB)]
        here = jnp.where(inside, (lane - base == sub).astype(jnp.float32), here)
        more = block + 1 < blocks
        if more:
            after = rows[block + 1]
            cols_after = [col(after, base + j) for j in range(SUB)]
            after = jnp.where(inside, 0.0, after)
        pivots = jnp.zeros((SUB, n), jnp.float32)
        scales = jnp.zeros((SUB, n), jnp.float32)
        for k in range(0, SUB, 2):
            a, b, c = row(cols[k], k), row(cols[k + 1], k), row(cols[k + 1], k + 1)
            det = a * c - b * b
            inv_a = pl.reciprocal(a)
            inv_det = pl.reciprocal(det)
            ratio = b * inv_a
            first = row(here, k)
            second = row(here, k + 1) - ratio * first
            m1 = jnp.where(sub > k, cols[k], 0.0) * inv_a
            m2 = jnp.where(sub > k + 1, a * cols[k + 1] - b * cols[k], 0.0) * inv_det
            if more:
                n1 = cols_after[k] * inv_a
                n2 = (a * cols_after[k + 1] - b * cols_after[k]) * inv_det
            pairs = [(row(cols[j], k), row(cols[j], k + 1)) for j in range(k + 2, SUB)]
            for j, (x1, x2) in zip(range(k + 2, SUB), pairs):
                x2 = x2 - ratio * x1
                cols[j] = cols[j] - m1 * x1 - m2 * x2
                if more:
                    cols_after[j] = cols_after[j] - n1 * x1 - n2 * x2
            here = here - m1 * first - m2 * second
            if more:
                after = after - n1 * first - n2 * second
            pivots = jnp.where(sub == k, a, jnp.where(sub == k + 1, det * inv_a, pivots))
            scales = jnp.where(sub == k, inv_a, jnp.where(sub == k + 1, a * inv_det, scales))
        if more:
            rows[block + 1] = after
        if block + 2 < blocks:
            rest = lax.dot_general(
                here * scales,
                here,
                (((0,), (0,)), ((), ())),
                precision=lax.Precision.HIGHEST,
                preferred_element_type=jnp.float32,
            )
            for i in range(block + 2, blocks):
                rows[i] = jnp.where(inside, 0.0, rows[i]) - rest[i * SUB : (i + 1) * SUB]
        out.append(jnp.where(lane <= sub + base, here * lax.rsqrt(pivots), 0.0))
    return out


def inverse_kernel(n_row, *refs):
    trailing, own, *others = refs[: 1 + n_row // 2]
    out, held, tile, sem = refs[1 + n_row // 2 :]
    load = pltpu.make_async_copy(trailing, held, sem)
    load.start()
    me = lax.axis_index("row")
    depth = own.shape[0] // 2
    for step, piece in zip(range(0, n_row, 2), (own, *others)):
        for half in range(2):
            start = pl.multiple_of((me ^ step ^ half) * depth, depth)
            tile[pl.ds(start, depth), :] = piece[half * depth : (half + 1) * depth, :]
    n = tile.shape[0]
    blocks = inverse_factor([tile[i * SUB : (i + 1) * SUB, :] for i in range(n // SUB)])
    for i in range(0, n // SUB, 2):
        pair = jnp.concatenate([blocks[i], blocks[i + 1]], 0)
        out[i * SUB : (i + 2) * SUB, :] = pair.astype(out.dtype)
    load.wait()


def product(a, b):
    return lax.dot_general(a, b, (((1,), (1,)), ((), ())), preferred_element_type=jnp.float32)


def update_kernel(n_col, *refs):
    inverse, col_panel = refs[:2]
    pieces = refs[2 : 2 + n_col]
    trailing, solved, updated = refs[2 + n_col : 5 + n_col]
    new, col_solved, out_sems = refs[5 + n_col :]
    row, col = lax.axis_index("row"), lax.axis_index("col")
    rows_dev, cols_dev = trailing.shape
    depth = pieces[0].shape[0]
    chunk = min(CHUNK, depth)
    per_piece = depth // chunk

    def start_of(step, part):
        return pl.multiple_of((col ^ step) * depth + part * chunk, chunk)

    def store(step, part):
        span = pl.ds(start_of(step, part), chunk)
        return pltpu.make_async_copy(
            new.at[span], updated.at[span], out_sems.at[step * per_piece + part]
        )

    order = [(step, part) for step in range(n_col) for part in range(per_piece)]
    weights = inverse[...]
    col_solved[...] = product(col_panel[...], weights).astype(col_solved.dtype)
    for step, part in order:
        span = slice(part * chunk, (part + 1) * chunk)
        rows = product(pieces[step][span, :], weights).astype(solved.dtype)
        if step == 0:
            solved[span, :] = rows
        start = start_of(step, part)
        place = pl.ds(start, chunk)
        first_row = row * rows_dev + start
        first_col = col * cols_dev
        update = product(rows, col_solved[...])

        @pl.when(first_row >= first_col + cols_dev)
        def _():
            new[place, :] = trailing[place, :] - update

        @pl.when(first_row < first_col + cols_dev)
        def _():
            row_ids = first_row + lax.broadcasted_iota(jnp.int32, (chunk, cols_dev), 0)
            col_ids = first_col + lax.broadcasted_iota(jnp.int32, (chunk, cols_dev), 1)
            new[place, :] = trailing[place, :] - jnp.where(row_ids >= col_ids, update, 0.0)

        store(step, part).start()
    for step, part in order:
        store(step, part).wait()


def column_rows(panel, n_row, n_col, cols_dev):
    depth = panel.shape[0]
    rows_dev = depth * n_col
    row, col = lax.axis_index("row"), lax.axis_index("col")
    if depth == cols_dev and n_col * cols_dev <= rows_dev:
        half = depth // 2
        odd = row % 2 == 1
        beside = exchange(panel, "row", n_row, 1)
        mine = jnp.where(odd, beside[half:], panel[:half])
        part = mine
        for step in far_steps(n_row):
            came = exchange(mine, "row", n_row, step)
            part = jnp.where(row // 2 == step // 2, came, part)
        other = exchange(part, "row", n_row, 1)
        return jnp.where(
            odd, jnp.concatenate([other, part], 0), jnp.concatenate([part, other], 0)
        )
    whole = lax.all_gather(panel, "col", axis=0, tiled=True)
    start = col * cols_dev
    picked = lax.dynamic_slice_in_dim(whole, start % rows_dev, cols_dev, 0)
    kept = jnp.where(row == start // rows_dev, picked, 0).astype(picked.dtype)
    return lax.psum(kept, "row")


def per_device(n_row, n_col, diag_tile, panel, trailing):
    rows_dev, cols_dev = trailing.shape
    depth, width = panel.shape
    pieces = [panel] + [exchange(panel, "col", n_col, step) for step in range(1, n_col)]
    beside = exchange(diag_tile, "row", n_row, 1)
    two = jnp.concatenate([diag_tile, beside], 0)
    far = [exchange(two, "row", n_row, 2 * i) for i in range(1, n_row // 2)]
    inverse, held = pl.pallas_call(
        functools.partial(inverse_kernel, n_row),
        out_shape=(
            jax.ShapeDtypeStruct((width, width), jnp.bfloat16),
            jax.ShapeDtypeStruct(trailing.shape, trailing.dtype),
        ),
        in_specs=[HBM] + [VMEM] * (n_row // 2),
        out_specs=(VMEM, VMEM),
        scratch_shapes=[
            pltpu.VMEM((width, width), jnp.float32),
            pltpu.SemaphoreType.DMA,
        ],
        cost_estimate=pl.CostEstimate(
            flops=2 * width**3, bytes_accessed=width * width * 6, transcendentals=width
        ),
        compiler_params=pltpu.CompilerParams(vmem_limit_bytes=8 * 1024 * 1024),
        name="inverse",
    )(trailing, two, *far)
    col_panel = column_rows(panel, n_row, n_col, cols_dev)
    chunks = n_col * (depth // min(CHUNK, depth))
    return pl.pallas_call(
        functools.partial(update_kernel, n_col),
        out_shape=(
            jax.ShapeDtypeStruct(panel.shape, panel.dtype),
            jax.ShapeDtypeStruct(trailing.shape, trailing.dtype),
        ),
        in_specs=[VMEM] * (3 + n_col),
        out_specs=(VMEM, HBM),
        scratch_shapes=[
            pltpu.VMEM(trailing.shape, trailing.dtype),
            pltpu.VMEM((cols_dev, width), panel.dtype),
            pltpu.SemaphoreType.DMA((chunks,)),
        ],
        compiler_params=pltpu.CompilerParams(vmem_limit_bytes=24 * 1024 * 1024),
        cost_estimate=pl.CostEstimate(
            flops=2 * rows_dev * cols_dev * width,
            bytes_accessed=2 * rows_dev * cols_dev * 4,
            transcendentals=0,
        ),
        name="update",
    )(inverse, col_panel, *pieces, held)


def solution(mesh):
    n_row, n_col = mesh.shape["row"], mesh.shape["col"]
    in_specs = (P("row", None), P(("row", "col"), None), P("row", "col"))
    out_specs = (P(("row", "col"), None), P("row", "col"))

    def step(*args):
        return per_device(n_row, n_col, *args)

    return jax.shard_map(
        step, mesh=mesh, in_specs=in_specs, out_specs=out_specs, check_vma=False
    )
```

time: 124 us -> 36 us (0.29)
  waiting for transfers between devices: 54.4 us -> 5.69 us
  blocking collectives: 26.2 us -> 0 us
  other arithmetic: 23.6 us -> 0.9 us
  starting transfers between devices: 0.04 us -> 16 us
  between operations: 14.1 us -> 0.73 us
  Pallas kernels: 0 us -> 9.57 us
  matrix products: 4.52 us -> 0 us
  local copies, waits for them, and re-layouts: 0.86 us -> 2.9 us
    psum x1 -> x0, waiting for transfers between devices: 54.4 us -> none  [from_root(): return lax.psum(kept, axis)]
    all_gather x2 -> x0, blocking collectives: 26.2 us -> none  [the longest x1 15.9 us: per_device(): whole_tile = lax.all_gather(diag_tile, 'row', axis=0, tiled=True)]
    another operation x5 -> x0, other arithmetic: 22.9 us -> none  [the longest x3 12.4 us: per_device(): factor = jnp.linalg.cholesky(whole_tile)]
    ppermute x0 -> x12, starting transfers between devices: none -> 16 us  [exchange(): return lax.ppermute(value, axis, [(i, i ^ step) for i in range(size)])]
    pallas_call x0 -> x2, Pallas kernels: none -> 9.57 us  [the longest x1 4.8 us: per_device(): pl.pallas_call(functools.partial(inverse_kernel, n_row), out_shape=(jax.S...]
    ppermute x0 -> x12, waiting for transfers between devices: none -> 5.69 us  [exchange(): return lax.ppermute(value, axis, [(i, i ^ step) for i in range(size)])]
    dot_general x2 -> x0, matrix products: 4.27 us -> none  [the longest x1 4.08 us: per_device(): lax.dot_general(row_panel, col_panel, (((1,), (1,)), ((), ())), preferred...]
    unnamed x3 -> x5, local copies, waits for them, and re-layouts: 0.77 us -> 2.89 us
  transfers between devices with their start and end apart: 1 -> 12, of which waited for: 1 -> 3; matrix products, arithmetic and copies ran while one was open for 1% -> 4% of each run, Pallas kernels for 0% -> 13%
where the time goes in v1:
time: 36 us; the launch traced here: 35.8 us
  starting transfers between devices  16 us (44%)
  Pallas kernels  9.57 us (27%)
  waiting for transfers between devices  5.69 us (16%)
  local copies, waits for them, and re-layouts  2.9 us (8%)
  other arithmetic  0.9 us (2%)
  between operations  0.73 us (2%)
    ppermute x12, starting transfers between devices, exchange(): return lax.ppermute(value, axis, [(i, i ^ step) for i in range(size)])  16 us
    ppermute x12, waiting for transfers between devices, exchange(): return lax.ppermute(value, axis, [(i, i ^ step) for i in range(size)])  5.69 us
    pallas_call x1, Pallas kernels, per_device(): pl.pallas_call(functools.partial(inverse_kernel, n_row), out_shape=(jax.S...  4.8 us
    pallas_call x1, Pallas kernels, per_device(): pl.pallas_call(functools.partial(update_kernel, n_col), out_shape=(jax.Sh...  4.77 us
    unnamed x5, local copies, waits for them, and re-layouts  2.89 us
    select_n x1, other arithmetic, column_rows(): mine = jnp.where(odd, beside[half:], panel[:half])  0.85 us
  transfers between devices with their start and end apart: 12, of which 3 were waited for; matrix products, arithmetic and copies ran while one was open for 4% of the time, Pallas kernels for 13%

profile of v1, /device:TPU:0, one launch (start us, length us, event | category | flops | bytes accessed | tf_op | source)
XLA Modules:
  0.0 35.8 jit_solution(12138370600548148265)
XLA Ops:
  0.6 0.0 copy-start.1
  0.6 0.6 %collective-permute-start.4 = (bf16[512,128]{1,0:T(8,128)(2,1)}, bf16[512,128]{1,0:T(8,128)(2,1)S(1)}, u32[]{:S(2)}, u32[]{:S(2)}) collective-permute-start(bf16[512,128]{1,0:T(8,128)(2,1)} %refs_2_.1), channel_id=1, source_target_pairs={{0,4},{4,0},{8,12},{12,8},{16,20},{20,16},{24,28},{28,24},{1,5},{5... | collective-permute-start | bytes 393224 | tf_op jit(solution)/shard_map/ppermute | solution.py:19
  1.2 0.1 collective-permute-start
  1.3 1.1 %collective-permute-done.4 = bf16[512,128]{1,0:T(8,128)(2,1)S(1)} collective-permute-done((bf16[512,128]{1,0:T(8,128)(2,1)}, bf16[512,128]{1,0:T(8,128)(2,1)S(1)}, u32[]{:S(2)}, u32[]{:S(2)}) %collective-permute-start.4) | collective-permute-done | bytes 131104 | tf_op jit(solution)/shard_map/ppermute | solution.py:19
  2.4 0.8 %slice_select_fusion = bf16[256,128]{1,0:T(8,128)(2,1)S(1)} fusion(bf16[512,128]{1,0:T(8,128)(2,1)S(1)} %collective-permute-done.4, bf16[512,128]{1,0:T(8,128)(2,1)} %refs_2_.1, pred[]{:T(512)S(6)} %eq.14), kind=kLoop, calls=%fused_computation.1 | loop fusion | flops 32768 | bytes 196609 | tf_op jit(solution)/shard_map/jit(_where)/select_n | solution.py:173
  3.2 5.0 %collective-permute-start.7 = (bf16[256,128]{1,0:T(8,128)(2,1)S(1)}, bf16[256,128]{1,0:T(8,128)(2,1)S(1)}, u32[]{:S(2)}, u32[]{:S(2)}) collective-permute-start(bf16[256,128]{1,0:T(8,128)(2,1)S(1)} %slice_select_fusion), channel_id=1, source_target_pairs={{0,24},{4,28},{8,16},{12,20},{16,8},{20,12},{24,0},{28,4},{1,25},{... | collective-permute-start | bytes 196616 | tf_op jit(solution)/shard_map/ppermute | solution.py:19
  8.3 0.0 collective-permute-start.6
  8.3 0.6 %collective-permute-start.5 = (bf16[256,128]{1,0:T(8,128)(2,1)S(1)}, bf16[256,128]{1,0:T(8,128)(2,1)S(1)}, u32[]{:S(2)}, u32[]{:S(2)}) collective-permute-start(bf16[256,128]{1,0:T(8,128)(2,1)S(1)} %slice_select_fusion), channel_id=1, source_target_pairs={{0,8},{4,12},{8,0},{12,4},{16,24},{20,28},{24,16},{28,20},{1,9},{5... | collective-permute-start | bytes 196616 | tf_op jit(solution)/shard_map/ppermute | solution.py:19
  8.9 0.7 %constant_dynamic-update-slice_fusion.1 = f32[32,128]{1,0:T(8,128)S(1)} fusion(f32[16,128]{1,0:T(8,128)} %param.3), kind=kLoop, calls=%fused_computation.4 | loop fusion | bytes 16384
  9.6 1.3 %collective-permute-done.7 = bf16[256,128]{1,0:T(8,128)(2,1)S(1)} collective-permute-done((bf16[256,128]{1,0:T(8,128)(2,1)S(1)}, bf16[256,128]{1,0:T(8,128)(2,1)S(1)}, u32[]{:S(2)}, u32[]{:S(2)}) %collective-permute-start.7) | collective-permute-done | bytes 65568 | tf_op jit(solution)/shard_map/ppermute | solution.py:19
  10.9 3.3 %collective-permute-done.6 = bf16[256,128]{1,0:T(8,128)(2,1)S(1)} collective-permute-done((bf16[256,128]{1,0:T(8,128)(2,1)S(1)}, bf16[256,128]{1,0:T(8,128)(2,1)S(1)}, u32[]{:S(2)}, u32[]{:S(2)}) %collective-permute-start.6) | collective-permute-done | bytes 65568 | tf_op jit(solution)/shard_map/ppermute | solution.py:19
  14.1 0.0 collective-permute-done.5
  14.2 0.1 collective-permute-start.8
  14.2 0.0 collective-permute-done
  14.3 2.5 %collective-permute-start.3 = (f32[32,128]{1,0:T(8,128)S(1)}, f32[32,128]{1,0:T(8,128)S(1)}, u32[]{:S(2)}, u32[]{:S(2)}) collective-permute-start(f32[32,128]{1,0:T(8,128)S(1)} %constant_dynamic-update-slice_fusion.refs_1_), channel_id=1, source_target_pairs={{0,24},{4,28},{8,16},{12,20},{16,8},{20,12},{24,0},{28,4},{1,25},{... | collective-permute-start | bytes 49160 | tf_op jit(solution)/shard_map/ppermute | solution.py:19
  16.8 0.1 collective-permute-start.2
  16.9 1.8 %collective-permute-start.1 = (f32[32,128]{1,0:T(8,128)S(1)}, f32[32,128]{1,0:T(8,128)S(1)}, u32[]{:S(2)}, u32[]{:S(2)}) collective-permute-start(f32[32,128]{1,0:T(8,128)S(1)} %constant_dynamic-update-slice_fusion.refs_1_), channel_id=1, source_target_pairs={{0,8},{4,12},{8,0},{12,4},{16,24},{20,28},{24,16},{28,20},{1,9},{5... | collective-permute-start | bytes 49160 | tf_op jit(solution)/shard_map/ppermute | solution.py:19
  18.7 1.5 %collective-permute-start.10 = (bf16[512,128]{1,0:T(8,128)(2,1)}, bf16[512,128]{1,0:T(8,128)(2,1)S(1)}, u32[]{:S(2)}, u32[]{:S(2)}) collective-permute-start(bf16[512,128]{1,0:T(8,128)(2,1)} %refs_2_.1), channel_id=1, source_target_pairs={{0,2},{1,3},{2,0},{3,1},{4,6},{5,7},{6,4},{7,5},{8,10},{9,11},{10,... | collective-permute-start | bytes 393224 | tf_op jit(solution)/shard_map/ppermute | solution.py:19
  20.2 0.0 collective-permute-done.3.refs_4_
  20.2 1.5 %collective-permute-start.9 = (bf16[512,128]{1,0:T(8,128)(2,1)}, bf16[512,128]{1,0:T(8,128)(2,1)S(1)}, u32[]{:S(2)}, u32[]{:S(2)}) collective-permute-start(bf16[512,128]{1,0:T(8,128)(2,1)} %refs_2_.1), channel_id=1, source_target_pairs={{0,1},{1,0},{2,3},{3,2},{4,5},{5,4},{6,7},{7,6},{8,9},{9,8},{10,11... | collective-permute-start | bytes 393224 | tf_op jit(solution)/shard_map/ppermute | solution.py:19
  21.7 0.0 collective-permute-done.2.refs_3_
  21.7 2.2 %collective-permute-start.11 = (bf16[512,128]{1,0:T(8,128)(2,1)}, bf16[512,128]{1,0:T(8,128)(2,1)S(1)}, u32[]{:S(2)}, u32[]{:S(2)}) collective-permute-start(bf16[512,128]{1,0:T(8,128)(2,1)} %refs_2_.1), channel_id=1, source_target_pairs={{0,3},{1,2},{2,1},{3,0},{4,7},{5,6},{6,5},{7,4},{8,11},{9,10},{10,... | collective-permute-start | bytes 393224 | tf_op jit(solution)/shard_map/ppermute | solution.py:19
  23.9 0.0 collective-permute-done.1.refs_2_
  23.9 0.0 copy-start
  23.9 2.2 %copy-done = f32[2048,512]{1,0:T(8,128)S(1)} copy-done((f32[2048,512]{1,0:T(8,128)S(1)}, f32[2048,512]{1,0:T(8,128)}, u32[]{:S(2)}) %copy-start) | copy-done | bytes 4194328
  26.1 4.8 %inverse.1 = (bf16[128,128]{1,0:T(8,128)(2,1)S(1)}, f32[2048,512]{1,0:T(8,128)S(1)}) custom-call(f32[2048,512]{1,0:T(8,128)S(1)} %copy-done, f32[32,128]{1,0:T(8,128)S(1)} %constant_dynamic-update-slice_fusion.refs_1_, f32[32,128]{1,0:T(8,128)S(1)} %collective-permute-done.1.refs_2_, f32[32,128]{1,0:T(8,128)S(1)} %collective-permute-done.2.refs_3_, ...), custom_call_target="tpu_custom_call" | custom-call | flops 4194304 | bytes 98304 | tf_op jit(solution)/shard_map/inverse/pallas_call | solution.py:196
  30.9 0.0 collective-permute-done.8
  31.0 0.0 collective-permute-done.10.refs_4_
  31.0 0.0 collective-permute-done.9.refs_3_
  31.0 0.0 collective-permute-done.11.refs_5_
  31.0 0.0 copy-done.1
  31.0 4.8 %update.1 = (bf16[512,128]{1,0:T(8,128)(2,1)}, f32[2048,512]{1,0:T(8,128)}) custom-call(bf16[128,128]{1,0:T(8,128)(2,1)S(1)} %get-tuple-element.4.refs_0_, bf16[512,128]{1,0:T(8,128)(2,1)S(1)} %maximum_select_fusion.refs_1_, bf16[512,128]{1,0:T(8,128)(2,1)S(1)} %copy-done.1, bf16[512,128]{1,0:T(8,128)(2,1)S(1)} %collective-permute-done.9.refs_3_, ...), custom_call_target="tpu_custom_call" | custom-call | flops 268435456 | bytes 8388608 | tf_op jit(solution)/shard_map/update/pallas_call | solution.py:216
  (3 shorter events, 0.1 us)
Async XLA Ops:
  0.6 30.4 %copy-start.1 = (bf16[512,128]{1,0:T(8,128)(2,1)S(1)}, bf16[512,128]{1,0:T(8,128)(2,1)}, u32[]{:S(2)}) copy-start(bf16[512,128]{1,0:T(8,128)(2,1)} %refs_2_.1) | copy-start | bytes 393220
  0.6 1.8 %collective-permute-start.4 = (bf16[512,128]{1,0:T(8,128)(2,1)}, bf16[512,128]{1,0:T(8,128)(2,1)S(1)}, u32[]{:S(2)}, u32[]{:S(2)}) collective-permute-start(bf16[512,128]{1,0:T(8,128)(2,1)} %refs_2_.1), channel_id=1, source_target_pairs={{0,4},{4,0},{8,12},{12,8},{16,20},{20,16},{24,28},{28,24},{1,5},{5... | collective-permute-start | bytes 393224 | tf_op jit(solution)/shard_map/ppermute | solution.py:19
  1.2 13.0 %collective-permute-start = (f32[16,128]{1,0:T(8,128)}, f32[16,128]{1,0:T(8,128)S(1)}, u32[]{:S(2)}, u32[]{:S(2)}) collective-permute-start(f32[16,128]{1,0:T(8,128)} %param.3), channel_id=1, source_target_pairs={{0,4},{4,0},{8,12},{12,8},{16,20},{20,16},{24,28},{28,24},{1,5},{5... | collective-permute-start | bytes 24584 | tf_op jit(solution)/shard_map/ppermute | solution.py:19
  3.2 7.6 %collective-permute-start.7 = (bf16[256,128]{1,0:T(8,128)(2,1)S(1)}, bf16[256,128]{1,0:T(8,128)(2,1)S(1)}, u32[]{:S(2)}, u32[]{:S(2)}) collective-permute-start(bf16[256,128]{1,0:T(8,128)(2,1)S(1)} %slice_select_fusion), channel_id=1, source_target_pairs={{0,24},{4,28},{8,16},{12,20},{16,8},{20,12},{24,0},{28,4},{1,25},{... | collective-permute-start | bytes 196616 | tf_op jit(solution)/shard_map/ppermute | solution.py:19
  8.3 5.9 %collective-permute-start.6 = (bf16[256,128]{1,0:T(8,128)(2,1)S(1)}, bf16[256,128]{1,0:T(8,128)(2,1)S(1)}, u32[]{:S(2)}, u32[]{:S(2)}) collective-permute-start(bf16[256,128]{1,0:T(8,128)(2,1)S(1)} %slice_select_fusion), channel_id=1, source_target_pairs={{0,16},{4,20},{8,24},{12,28},{16,0},{20,4},{24,8},{28,12},{1,17},{... | collective-permute-start | bytes 196616 | tf_op jit(solution)/shard_map/ppermute | solution.py:19
  8.3 5.9 %collective-permute-start.5 = (bf16[256,128]{1,0:T(8,128)(2,1)S(1)}, bf16[256,128]{1,0:T(8,128)(2,1)S(1)}, u32[]{:S(2)}, u32[]{:S(2)}) collective-permute-start(bf16[256,128]{1,0:T(8,128)(2,1)S(1)} %slice_select_fusion), channel_id=1, source_target_pairs={{0,8},{4,12},{8,0},{12,4},{16,24},{20,28},{24,16},{28,20},{1,9},{5... | collective-permute-start | bytes 196616 | tf_op jit(solution)/shard_map/ppermute | solution.py:19
  14.2 16.7 %collective-permute-start.8 = (bf16[256,128]{1,0:T(8,128)(2,1)S(1)}, bf16[256,128]{1,0:T(8,128)(2,1)S(1)}, u32[]{:S(2)}, u32[]{:S(2)}) collective-permute-start(bf16[256,128]{1,0:T(8,128)(2,1)S(1)} %select_select_fusion), channel_id=1, source_target_pairs={{0,4},{4,0},{8,12},{12,8},{16,20},{20,16},{24,28},{28,24},{1,5},{5... | collective-permute-start | bytes 196616 | tf_op jit(solution)/shard_map/ppermute | solution.py:19
  14.3 6.0 %collective-permute-start.3 = (f32[32,128]{1,0:T(8,128)S(1)}, f32[32,128]{1,0:T(8,128)S(1)}, u32[]{:S(2)}, u32[]{:S(2)}) collective-permute-start(f32[32,128]{1,0:T(8,128)S(1)} %constant_dynamic-update-slice_fusion.refs_1_), channel_id=1, source_target_pairs={{0,24},{4,28},{8,16},{12,20},{16,8},{20,12},{24,0},{28,4},{1,25},{... | collective-permute-start | bytes 49160 | tf_op jit(solution)/shard_map/ppermute | solution.py:19
  16.8 4.9 %collective-permute-start.2 = (f32[32,128]{1,0:T(8,128)S(1)}, f32[32,128]{1,0:T(8,128)S(1)}, u32[]{:S(2)}, u32[]{:S(2)}) collective-permute-start(f32[32,128]{1,0:T(8,128)S(1)} %constant_dynamic-update-slice_fusion.refs_1_), channel_id=1, source_target_pairs={{0,16},{4,20},{8,24},{12,28},{16,0},{20,4},{24,8},{28,12},{1,17},{... | collective-permute-start | bytes 49160 | tf_op jit(solution)/shard_map/ppermute | solution.py:19
  16.9 7.0 %collective-permute-start.1 = (f32[32,128]{1,0:T(8,128)S(1)}, f32[32,128]{1,0:T(8,128)S(1)}, u32[]{:S(2)}, u32[]{:S(2)}) collective-permute-start(f32[32,128]{1,0:T(8,128)S(1)} %constant_dynamic-update-slice_fusion.refs_1_), channel_id=1, source_target_pairs={{0,8},{4,12},{8,0},{12,4},{16,24},{20,28},{24,16},{28,20},{1,9},{5... | collective-permute-start | bytes 49160 | tf_op jit(solution)/shard_map/ppermute | solution.py:19
  18.7 12.2 %collective-permute-start.10 = (bf16[512,128]{1,0:T(8,128)(2,1)}, bf16[512,128]{1,0:T(8,128)(2,1)S(1)}, u32[]{:S(2)}, u32[]{:S(2)}) collective-permute-start(bf16[512,128]{1,0:T(8,128)(2,1)} %refs_2_.1), channel_id=1, source_target_pairs={{0,2},{1,3},{2,0},{3,1},{4,6},{5,7},{6,4},{7,5},{8,10},{9,11},{10,... | collective-permute-start | bytes 393224 | tf_op jit(solution)/shard_map/ppermute | solution.py:19
  20.2 10.7 %collective-permute-start.9 = (bf16[512,128]{1,0:T(8,128)(2,1)}, bf16[512,128]{1,0:T(8,128)(2,1)S(1)}, u32[]{:S(2)}, u32[]{:S(2)}) collective-permute-start(bf16[512,128]{1,0:T(8,128)(2,1)} %refs_2_.1), channel_id=1, source_target_pairs={{0,1},{1,0},{2,3},{3,2},{4,5},{5,4},{6,7},{7,6},{8,9},{9,8},{10,11... | collective-permute-start | bytes 393224 | tf_op jit(solution)/shard_map/ppermute | solution.py:19
  21.7 9.2 %collective-permute-start.11 = (bf16[512,128]{1,0:T(8,128)(2,1)}, bf16[512,128]{1,0:T(8,128)(2,1)S(1)}, u32[]{:S(2)}, u32[]{:S(2)}) collective-permute-start(bf16[512,128]{1,0:T(8,128)(2,1)} %refs_2_.1), channel_id=1, source_target_pairs={{0,3},{1,2},{2,1},{3,0},{4,7},{5,6},{6,5},{7,4},{8,11},{9,10},{10,... | collective-permute-start | bytes 393224 | tf_op jit(solution)/shard_map/ppermute | solution.py:19
  23.9 2.2 %copy-start = (f32[2048,512]{1,0:T(8,128)S(1)}, f32[2048,512]{1,0:T(8,128)}, u32[]{:S(2)}) copy-start(f32[2048,512]{1,0:T(8,128)} %refs_0_.1) | copy-start | bytes 12582916

commit v2 on v1

v2 whole, which is shorter than its diff:
```python
import functools

import jax
import jax.numpy as jnp
from jax import lax
from jax.experimental import pallas as pl
from jax.experimental.pallas import tpu as pltpu
from jax.sharding import PartitionSpec as P


SUB = 8
CHUNK = 512

VMEM = pl.BlockSpec(memory_space=pltpu.VMEM)
HBM = pl.BlockSpec(memory_space=pltpu.HBM)


def exchange(value, axis, size, step):
    return lax.ppermute(value, axis, [(i, i ^ step) for i in range(size)])


def far_steps(n_row):
    return [2 * i for i in reversed(range(1, n_row // 2))]


def inverse_factor(tile):
    n = tile[0].shape[1]
    blocks = n // SUB
    rows = list(tile)
    lane = lax.broadcasted_iota(jnp.int32, (SUB, n), 1)
    sub = lax.broadcasted_iota(jnp.int32, (SUB, n), 0)

    def col(x, c):
        return jnp.broadcast_to(x[:, c : c + 1], (SUB, n))

    def row(x, r):
        return jnp.broadcast_to(x[r : r + 1, :], (SUB, n))

    out = []
    for block in range(blocks):
        base = block * SUB
        inside = (lane >= base) & (lane < base + SUB)
        here = rows[block]
        cols = [col(here, base + j) for j in range(SUB)]
        here = jnp.where(inside, (lane - base == sub).astype(jnp.float32), here)
        more = block + 1 < blocks
        if more:
            after = rows[block + 1]
            cols_after = [col(after, base + j) for j in range(SUB)]
            after = jnp.where(inside, 0.0, after)
        pivots = jnp.zeros((SUB, n), jnp.float32)
        scales = jnp.zeros((SUB, n), jnp.float32)
        for k in range(0, SUB, 2):
            a, b, c = row(cols[k], k), row(cols[k + 1], k), row(cols[k + 1], k + 1)
            det = a * c - b * b
            inv_a = pl.reciprocal(a)
            inv_det = pl.reciprocal(det)
            ratio = b * inv_a
            first = row(here, k)
            second = row(here, k + 1) - ratio * first
            m1 = jnp.where(sub > k, cols[k], 0.0) * inv_a
            m2 = jnp.where(sub > k + 1, a * cols[k + 1] - b * cols[k], 0.0) * inv_det
            if more:
                n1 = cols_after[k] * inv_a
                n2 = (a * cols_after[k + 1] - b * cols_after[k]) * inv_det
            pairs = [(row(cols[j], k), row(cols[j], k + 1)) for j in range(k + 2, SUB)]
            for j, (x1, x2) in zip(range(k + 2, SUB), pairs):
                x2 = x2 - ratio * x1
                cols[j] = cols[j] - m1 * x1 - m2 * x2
                if more:
                    cols_after[j] = cols_after[j] - n1 * x1 - n2 * x2
            here = here - m1 * first - m2 * second
            if more:
                after = after - n1 * first - n2 * second
            pivots = jnp.where(sub == k, a, jnp.where(sub == k + 1, det * inv_a, pivots))
            scales = jnp.where(sub == k, inv_a, jnp.where(sub == k + 1, a * inv_det, scales))
        if more:
            rows[block + 1] = after
        if block + 2 < blocks:
            rest = lax.dot_general(
                here * scales,
                here,
                (((0,), (0,)), ((), ())),
                precision=lax.Precision.HIGHEST,
                preferred_element_type=jnp.float32,
            )
            for i in range(block + 2, blocks):
                rows[i] = jnp.where(inside, 0.0, rows[i]) - rest[i * SUB : (i + 1) * SUB]
        out.append(jnp.where(lane <= sub + base, here * lax.rsqrt(pivots), 0.0))
    return out


def load_kernel(*refs):
    n = len(refs) // 2
    sems = refs[-1]
    copies = [
        pltpu.make_async_copy(refs[i], refs[n + i], sems.at[i]) for i in range(n)
    ]
    for copy in copies:
        copy.start()
    for copy in copies:
        copy.wait()


def pack_kernel(half, *refs):
    tile, tile_beside, *panels, out = refs
    me = lax.axis_index("row")
    odd = lax.rem(me, 2) == 1
    if half:
        panel, panel_beside = panels
        out[:half, :] = jnp.where(odd, panel_beside[half:, :], panel[:half, :])
    depth = tile.shape[0]
    for i, ref in enumerate((tile, tile_beside)):
        rest = ref[...]
        for term in range(3):
            start = half + (2 * term + i) * depth
            value = rest.astype(jnp.bfloat16)
            out[start : start + depth, :] = value
            rest = rest - value.astype(jnp.float32)


def inverse_kernel(n_row, half, *refs):
    trailing, *packs = refs[: 1 + n_row // 2]
    if half:
        near, out, held, tile, sem = refs[1 + n_row // 2 :]
    else:
        out, held, tile, sem = refs[1 + n_row // 2 :]
    load = pltpu.make_async_copy(trailing, held, sem)
    load.start()
    me = lax.axis_index("row")
    depth = tile.shape[0] // n_row
    for step, pack in zip(range(0, n_row, 2), packs):
        for i in range(2):
            terms = []
            for term in range(3):
                start = half + (2 * term + i) * depth
                terms.append(pack[start : start + depth, :].astype(jnp.float32))
            place = pl.multiple_of((me ^ step ^ i) * depth, depth)
            tile[pl.ds(place, depth), :] = (terms[0] + terms[1]) + terms[2]
        if half:

            @pl.when(me - lax.rem(me, 2) == step)
            def _():
                near[...] = pack[:half, :]

    @pl.when(me >= 0)
    def _():
        n = tile.shape[0]
        blocks = inverse_factor([tile[i * SUB : (i + 1) * SUB, :] for i in range(n // SUB)])
        for i in range(0, n // SUB, 2):
            pair = jnp.concatenate([blocks[i], blocks[i + 1]], 0)
            out[i * SUB : (i + 2) * SUB, :] = pair.astype(out.dtype)

    load.wait()


def product(a, b):
    return lax.dot_general(a, b, (((1,), (1,)), ((), ())), preferred_element_type=jnp.float32)


def update_kernel(n_col, first_half, *refs):
    if first_half:
        inverse, col_rows, held, *pieces = refs[: 3 + n_col]
        solved, solved_all, updated, new, col_solved, sems, own_sem = refs[3 + n_col :]
    else:
        inverse, col_rows, held, solved_all, _, updated, new, col_solved, sems, _ = refs
    row, col = lax.axis_index("row"), lax.axis_index("col")
    rows_dev, cols_dev = held.shape
    width = cols_dev // 2
    odd = lax.rem(row, 2)
    lanes = pl.multiple_of((odd if first_half else 1 - odd) * width, width)
    weights = inverse[...]
    col_solved[...] = product(col_rows[...], weights).astype(col_solved.dtype)
    if first_half:
        depth = pieces[0].shape[0]
        for step in range(n_col):
            place = pl.ds(pl.multiple_of((col ^ step) * depth, depth), depth)
            rows = product(pieces[step][...], weights)
            solved_all[place, :] = rows.astype(solved_all.dtype)
        own = pl.ds(pl.multiple_of(col * depth, depth), depth)
        save = pltpu.make_async_copy(solved_all.at[own], solved, own_sem)
        save.start()
    chunk = min(CHUNK, rows_dev)
    chunks = rows_dev // chunk
    ahead = row * rows_dev - (col * cols_dev + lanes)

    def store(i):
        place = pl.ds(pl.multiple_of(i * chunk, chunk), chunk)
        return pltpu.make_async_copy(
            new.at[place], updated.at[place, pl.ds(lanes, width)], sems.at[i]
        )

    @pl.loop(0, chunks)
    def _(i):
        start = pl.multiple_of(i * chunk, chunk)
        place = pl.ds(start, chunk)
        update = product(solved_all[place, :], col_solved[...])
        row_ids = lax.broadcasted_iota(jnp.int32, (chunk, width), 0)
        col_ids = lax.broadcasted_iota(jnp.int32, (chunk, width), 1)
        lower = col_ids - row_ids <= ahead + start
        old = held[place, pl.ds(lanes, width)]
        new[place, :] = old - jnp.where(lower, update, 0.0)
        store(i).start()

    @pl.loop(0, chunks)
    def _(i):
        store(i).wait()

    if first_half:
        save.wait()


def column_rows(panel, n_col, cols_dev):
    rows_dev = panel.shape[0] * n_col
    row, start = lax.axis_index("row"), lax.axis_index("col") * cols_dev
    whole = lax.all_gather(panel, "col", axis=0, tiled=True)
    picked = lax.dynamic_slice_in_dim(whole, start % rows_dev, cols_dev, 0)
    kept = jnp.where(row == start // rows_dev, picked, 0).astype(picked.dtype)
    rows = lax.psum(kept, "row")
    half = cols_dev // 2
    odd = row % 2 == 1
    return jnp.where(odd, rows[half:], rows[:half]), jnp.where(odd, rows[:half], rows[half:])


def per_device(n_row, n_col, diag_tile, panel, trailing):
    rows_dev, cols_dev = trailing.shape
    depth, width = panel.shape
    direct = depth == cols_dev and n_col * cols_dev <= rows_dev
    half = depth // 2 if direct else 0
    pieces = []
    for step in range(1, n_col):
        pieces.append(exchange(panel, "col", n_col, step))
    tile_near, panel_near = pl.pallas_call(
        load_kernel,
        out_shape=[jax.ShapeDtypeStruct(a.shape, a.dtype) for a in (diag_tile, panel)],
        in_specs=[HBM] * 2,
        out_specs=[VMEM] * 2,
        scratch_shapes=[pltpu.SemaphoreType.DMA((2,))],
        cost_estimate=pl.CostEstimate(flops=1, bytes_accessed=4 * depth * width, transcendentals=0),
        compiler_params=pltpu.CompilerParams(vmem_limit_bytes=4 * 1024 * 1024),
        name="load",
    )(diag_tile, panel)
    packed = [tile_near, exchange(diag_tile, "row", n_row, 1)]
    if direct:
        packed += [panel_near, exchange(panel, "row", n_row, 1)]
    pieces.insert(0, panel_near)
    pack_shape = (half + 6 * diag_tile.shape[0], width)
    pack = pl.pallas_call(
        functools.partial(pack_kernel, half),
        out_shape=jax.ShapeDtypeStruct(pack_shape, jnp.bfloat16),
        in_specs=[VMEM] * len(packed),
        out_specs=VMEM,
        cost_estimate=pl.CostEstimate(flops=1, bytes_accessed=4 * half * width, transcendentals=0),
        compiler_params=pltpu.CompilerParams(vmem_limit_bytes=4 * 1024 * 1024),
        name="pack",
    )(*packed)
    packs = {0: pack}
    for step in far_steps(n_row):
        packs[step] = exchange(pack, "row", n_row, step)
    packs = [packs[step] for step in range(0, n_row, 2)]
    outs = [
        jax.ShapeDtypeStruct((width, width), jnp.bfloat16),
        jax.ShapeDtypeStruct(trailing.shape, trailing.dtype),
    ]
    if direct:
        outs = [jax.ShapeDtypeStruct((half, width), panel.dtype)] + outs
    *near, inverse, held = pl.pallas_call(
        functools.partial(inverse_kernel, n_row, half),
        out_shape=outs,
        in_specs=[HBM] + [VMEM] * (n_row // 2),
        out_specs=[VMEM] * len(outs),
        scratch_shapes=[
            pltpu.VMEM((width, width), jnp.float32),
            pltpu.SemaphoreType.DMA,
        ],
        cost_estimate=pl.CostEstimate(
            flops=2 * width**3, bytes_accessed=width * width * 6, transcendentals=width
        ),
        compiler_params=pltpu.CompilerParams(vmem_limit_bytes=48 * 1024 * 1024),
        name="inverse",
    )(trailing, *packs)
    if direct:
        near = near[0]
        other = exchange(near, "row", n_row, 1)
    else:
        near, other = column_rows(panel, n_col, cols_dev)
    chunks = rows_dev // min(CHUNK, rows_dev)

    def update(first_half, operands, outs, out_specs, aliases):
        return pl.pallas_call(
            functools.partial(update_kernel, n_col, first_half),
            out_shape=outs,
            in_specs=[VMEM] * (len(operands) - len(aliases)) + [HBM] * len(aliases),
            out_specs=out_specs,
            scratch_shapes=[
                pltpu.VMEM((rows_dev, cols_dev // 2), trailing.dtype),
                pltpu.VMEM((cols_dev // 2, width), panel.dtype),
                pltpu.SemaphoreType.DMA((chunks,)),
                pltpu.SemaphoreType.DMA,
            ],
            input_output_aliases=aliases,
            compiler_params=pltpu.CompilerParams(vmem_limit_bytes=16 * 1024 * 1024),
            cost_estimate=pl.CostEstimate(
                flops=rows_dev * cols_dev * width,
                bytes_accessed=rows_dev * cols_dev * 4,
                transcendentals=0,
            ),
            name="update_first" if first_half else "update_second",
        )(*operands)

    slab = jax.ShapeDtypeStruct(trailing.shape, trailing.dtype)
    own = jax.ShapeDtypeStruct(panel.shape, panel.dtype)
    block = jax.ShapeDtypeStruct((rows_dev, width), panel.dtype)
    solved, solved_all, updated = update(
        True, (inverse, near, held, *pieces), (own, block, slab), (HBM, VMEM, HBM), {}
    )
    updated = update(
        False, (inverse, other, held, solved_all, updated), slab, HBM, {4: 0}
    )
    return solved, updated


def solution(mesh):
    n_row, n_col = mesh.shape["row"], mesh.shape["col"]
    in_specs = (P("row", None), P(("row", "col"), None), P("row", "col"))
    out_specs = (P(("row", "col"), None), P("row", "col"))

    def step(*args):
        return per_device(n_row, n_col, *args)

    return jax.shard_map(
        step, mesh=mesh, in_specs=in_specs, out_specs=out_specs, check_vma=False
    )
```

time: 36 us -> 25 us (0.69)
  starting transfers between devices: 16 us -> 9.84 us
  local copies, waits for them, and re-layouts: 2.9 us -> 0.7 us
  waiting for transfers between devices: 5.69 us -> 3.98 us
  other arithmetic: 0.9 us -> 0 us
    ppermute x12 -> x9, starting transfers between devices: 16 us -> 9.84 us  [exchange(): return lax.ppermute(value, axis, [(i, i ^ step) for i in range(size)])]
    unnamed x5 -> x2, local copies, waits for them, and re-layouts: 2.89 us -> 0.7 us
    ppermute x12 -> x9, waiting for transfers between devices: 5.69 us -> 3.98 us  [exchange(): return lax.ppermute(value, axis, [(i, i ^ step) for i in range(size)])]
    select_n x3 -> x0, other arithmetic: 0.9 us -> none  [the longest x1 0.85 us: column_rows(): mine = jnp.where(odd, beside[half:], panel[:half])]
    pallas_call x2 -> x5, Pallas kernels: 9.57 us -> 9.51 us  [the longest x1 4.54 us: per_device(): pl.pallas_call(functools.partial(inverse_kernel, n_row, half), out_shape=...]
  transfers between devices with their start and end apart: 12 -> 9, of which waited for: 3 -> 1; matrix products, arithmetic and copies ran while one was open for 4% -> 0% of each run, Pallas kernels for 13% -> 31%
where the time goes in v2:
time: 25 us; the launch traced here: 24.7 us
  starting transfers between devices  9.84 us (39%)
  Pallas kernels  9.51 us (38%)
  waiting for transfers between devices  3.98 us (16%)
  between operations  0.72 us (3%)
  local copies, waits for them, and re-layouts  0.7 us (3%)
    ppermute x9, starting transfers between devices, exchange(): return lax.ppermute(value, axis, [(i, i ^ step) for i in range(size)])  9.84 us
    pallas_call x1, Pallas kernels, per_device(): pl.pallas_call(functools.partial(inverse_kernel, n_row, half), out_shape=...  4.54 us
    pallas_call x2, Pallas kernels, update(): pl.pallas_call(functools.partial(update_kernel, n_col, first_half), out_s...  4.02 us
    ppermute x9, waiting for transfers between devices, exchange(): return lax.ppermute(value, axis, [(i, i ^ step) for i in range(size)])  3.98 us
    pallas_call x1, Pallas kernels, per_device(): pl.pallas_call(load_kernel, out_shape=[jax.ShapeDtypeStruct(a.shape, a.dt...  0.92 us
    unnamed x2, local copies, waits for them, and re-layouts  0.7 us
  transfers between devices with their start and end apart: 9, of which 1 were waited for; matrix products, arithmetic and copies ran while one was open for 0% of the time, Pallas kernels for 31%

profile of v2, /device:TPU:0, one launch (start us, length us, event | category | flops | bytes accessed | tf_op | source)
XLA Modules:
  0.0 24.7 jit_solution(14837413510357427297)
XLA Ops:
  0.6 0.6 %collective-permute-start.1 = (bf16[512,128]{1,0:T(8,128)(2,1)}, bf16[512,128]{1,0:T(8,128)(2,1)S(1)}, u32[]{:S(2)}, u32[]{:S(2)}) collective-permute-start(bf16[512,128]{1,0:T(8,128)(2,1)} %refs_1_.1), channel_id=1, source_target_pairs={{0,4},{4,0},{8,12},{12,8},{16,20},{20,16},{24,28},{28,24},{1,5},{5... | collective-permute-start | bytes 393224 | tf_op jit(solution)/shard_map/ppermute | solution.py:19
  1.2 0.1 collective-permute-start
  1.3 0.0 copy-start
  1.3 0.7 %copy-done = f32[16,128]{1,0:T(8,128)S(1)} copy-done((f32[16,128]{1,0:T(8,128)S(1)}, f32[16,128]{1,0:T(8,128)}, u32[]{:S(2)}) %copy-start) | copy-done | bytes 8216
  2.0 0.9 %load.1 = (f32[16,128]{1,0:T(8,128)S(1)}, bf16[512,128]{1,0:T(8,128)(2,1)S(1)}) custom-call(f32[16,128]{1,0:T(8,128)S(1)} %copy-done, bf16[512,128]{1,0:T(8,128)(2,1)} %refs_1_.1), custom_call_target="tpu_custom_call" | custom-call | flops 1 | bytes 262144 | tf_op jit(solution)/shard_map/load/pallas_call | solution.py:233
  2.9 0.0 collective-permute-done.refs_1_
  2.9 0.0 collective-permute-done.1.refs_3_
  3.0 3.1 %collective-permute-start.2 = (bf16[352,128]{1,0:T(8,128)(2,1)S(1)}, bf16[352,128]{1,0:T(8,128)(2,1)S(1)}, u32[]{:S(2)}, u32[]{:S(2)}) collective-permute-start(bf16[352,128]{1,0:T(8,128)(2,1)S(1)} %pack.1.refs_1_), channel_id=1, source_target_pairs={{0,8},{4,12},{8,0},{12,4},{16,24},{20,28},{24,16},{28,20},{1,9},{5... | collective-permute-start | bytes 270344 | tf_op jit(solution)/shard_map/ppermute | solution.py:19
  6.0 2.6 %collective-permute-start.3 = (bf16[352,128]{1,0:T(8,128)(2,1)S(1)}, bf16[352,128]{1,0:T(8,128)(2,1)S(1)}, u32[]{:S(2)}, u32[]{:S(2)}) collective-permute-start(bf16[352,128]{1,0:T(8,128)(2,1)S(1)} %pack.1.refs_1_), channel_id=1, source_target_pairs={{0,16},{4,20},{8,24},{12,28},{16,0},{20,4},{24,8},{28,12},{1,17},{... | collective-permute-start | bytes 270344 | tf_op jit(solution)/shard_map/ppermute | solution.py:19
  8.6 0.0 collective-permute-start.4
  8.6 1.7 %collective-permute-start.5 = (bf16[512,128]{1,0:T(8,128)(2,1)}, bf16[512,128]{1,0:T(8,128)(2,1)S(1)}, u32[]{:S(2)}, u32[]{:S(2)}) collective-permute-start(bf16[512,128]{1,0:T(8,128)(2,1)} %refs_1_.1), channel_id=1, source_target_pairs={{0,1},{1,0},{2,3},{3,2},{4,5},{5,4},{6,7},{7,6},{8,9},{9,8},{10,11... | collective-permute-start | bytes 393224 | tf_op jit(solution)/shard_map/ppermute | solution.py:19
  10.3 1.5 %collective-permute-start.6 = (bf16[512,128]{1,0:T(8,128)(2,1)}, bf16[512,128]{1,0:T(8,128)(2,1)S(1)}, u32[]{:S(2)}, u32[]{:S(2)}) collective-permute-start(bf16[512,128]{1,0:T(8,128)(2,1)} %refs_1_.1), channel_id=1, source_target_pairs={{0,2},{1,3},{2,0},{3,1},{4,6},{5,7},{6,4},{7,5},{8,10},{9,11},{10,... | collective-permute-start | bytes 393224 | tf_op jit(solution)/shard_map/ppermute | solution.py:19
  11.8 0.0 collective-permute-done.2.refs_2_
  11.8 0.3 %collective-permute-start.7 = (bf16[512,128]{1,0:T(8,128)(2,1)}, bf16[512,128]{1,0:T(8,128)(2,1)S(1)}, u32[]{:S(2)}, u32[]{:S(2)}) collective-permute-start(bf16[512,128]{1,0:T(8,128)(2,1)} %refs_1_.1), channel_id=1, source_target_pairs={{0,3},{1,2},{2,1},{3,0},{4,7},{5,6},{6,5},{7,4},{8,11},{9,10},{10,... | collective-permute-start | bytes 393224 | tf_op jit(solution)/shard_map/ppermute | solution.py:19
  12.1 4.0 %collective-permute-done.3.refs_3_ = bf16[352,128]{1,0:T(8,128)(2,1)S(1)} collective-permute-done((bf16[352,128]{1,0:T(8,128)(2,1)S(1)}, bf16[352,128]{1,0:T(8,128)(2,1)S(1)}, u32[]{:S(2)}, u32[]{:S(2)}) %collective-permute-start.3) | collective-permute-done | bytes 90144 | tf_op jit(solution)/shard_map/ppermute | solution.py:19
  16.0 0.0 collective-permute-done.4.refs_4_
  16.0 4.5 %inverse.1 = (bf16[256,128]{1,0:T(8,128)(2,1)S(1)}, bf16[128,128]{1,0:T(8,128)(2,1)S(1)}, f32[2048,512]{1,0:T(8,128)S(1)}) custom-call(f32[2048,512]{1,0:T(8,128)} %refs_0_.3, bf16[352,128]{1,0:T(8,128)(2,1)S(1)} %pack.1.refs_1_, bf16[352,128]{1,0:T(8,128)(2,1)S(1)} %collective-permute-done.2.refs_2_, bf16[352,128]{1,0:T(8,128)(2,1)S(1)} %collective-permute-done.3.refs_3_, ...), custom_call_target="tpu_custom_call" | custom-call | flops 4194304 | bytes 98304 | tf_op jit(solution)/shard_map/inverse/pallas_call | solution.py:267
  20.6 0.1 collective-permute-start.8
  20.7 0.0 collective-permute-done.5.refs_4_
  20.7 0.0 collective-permute-done.6.refs_5_
  20.7 0.0 collective-permute-done.7.refs_6_
  20.7 2.1 %update_first.1 = (bf16[512,128]{1,0:T(8,128)(2,1)}, bf16[2048,128]{1,0:T(8,128)(2,1)S(1)}, f32[2048,512]{1,0:T(8,128)}) custom-call(bf16[128,128]{1,0:T(8,128)(2,1)S(1)} %get-tuple-element.12.refs_0_, bf16[256,128]{1,0:T(8,128)(2,1)S(1)} %get-tuple-element.13.refs_1_, f32[2048,512]{1,0:T(8,128)S(1)} %get-tuple-element.14.refs_2_, ...), custom_call_target="tpu_custom_call" | custom-call | flops 134217728 | bytes 4194304 | tf_op jit(solution)/shard_map/update_first/pallas_call | solution.py:290
  22.8 0.0 collective-permute-done.8.refs_1_
  22.8 1.9 %update_second.1 = f32[2048,512]{1,0:T(8,128)} custom-call(bf16[128,128]{1,0:T(8,128)(2,1)S(1)} %get-tuple-element.12.refs_0_, bf16[256,128]{1,0:T(8,128)(2,1)S(1)} %collective-permute-done.8.refs_1_, f32[2048,512]{1,0:T(8,128)S(1)} %get-tuple-element.14.refs_2_, bf16[2048,128]{1,0:T(8,128)(2,1)S(1)} %get-tuple-element.16.refs_3_, ...), custom_call_target="tpu_custom_call", output_to_operand_aliasing={{}: (4, {})} | custom-call | flops 134217728 | bytes 4194304 | tf_op jit(solution)/shard_map/update_second/pallas_call | solution.py:290
  (1 shorter events, 0.0 us)
Async XLA Ops:
  0.6 2.3 %collective-permute-start.1 = (bf16[512,128]{1,0:T(8,128)(2,1)}, bf16[512,128]{1,0:T(8,128)(2,1)S(1)}, u32[]{:S(2)}, u32[]{:S(2)}) collective-permute-start(bf16[512,128]{1,0:T(8,128)(2,1)} %refs_1_.1), channel_id=1, source_target_pairs={{0,4},{4,0},{8,12},{12,8},{16,20},{20,16},{24,28},{28,24},{1,5},{5... | collective-permute-start | bytes 393224 | tf_op jit(solution)/shard_map/ppermute | solution.py:19
  1.2 1.7 %collective-permute-start = (f32[16,128]{1,0:T(8,128)}, f32[16,128]{1,0:T(8,128)S(1)}, u32[]{:S(2)}, u32[]{:S(2)}) collective-permute-start(f32[16,128]{1,0:T(8,128)} %refs_0_.2), channel_id=1, source_target_pairs={{0,4},{4,0},{8,12},{12,8},{16,20},{20,16},{24,28},{28,24},{1,5},{5... | collective-permute-start | bytes 24584 | tf_op jit(solution)/shard_map/ppermute | solution.py:19
  1.3 0.7 %copy-start = (f32[16,128]{1,0:T(8,128)S(1)}, f32[16,128]{1,0:T(8,128)}, u32[]{:S(2)}) copy-start(f32[16,128]{1,0:T(8,128)} %refs_0_.2) | copy-start | bytes 24580
  3.0 8.9 %collective-permute-start.2 = (bf16[352,128]{1,0:T(8,128)(2,1)S(1)}, bf16[352,128]{1,0:T(8,128)(2,1)S(1)}, u32[]{:S(2)}, u32[]{:S(2)}) collective-permute-start(bf16[352,128]{1,0:T(8,128)(2,1)S(1)} %pack.1.refs_1_), channel_id=1, source_target_pairs={{0,8},{4,12},{8,0},{12,4},{16,24},{20,28},{24,16},{28,20},{1,9},{5... | collective-permute-start | bytes 270344 | tf_op jit(solution)/shard_map/ppermute | solution.py:19
  6.0 10.0 %collective-permute-start.3 = (bf16[352,128]{1,0:T(8,128)(2,1)S(1)}, bf16[352,128]{1,0:T(8,128)(2,1)S(1)}, u32[]{:S(2)}, u32[]{:S(2)}) collective-permute-start(bf16[352,128]{1,0:T(8,128)(2,1)S(1)} %pack.1.refs_1_), channel_id=1, source_target_pairs={{0,16},{4,20},{8,24},{12,28},{16,0},{20,4},{24,8},{28,12},{1,17},{... | collective-permute-start | bytes 270344 | tf_op jit(solution)/shard_map/ppermute | solution.py:19
  8.6 7.5 %collective-permute-start.4 = (bf16[352,128]{1,0:T(8,128)(2,1)S(1)}, bf16[352,128]{1,0:T(8,128)(2,1)S(1)}, u32[]{:S(2)}, u32[]{:S(2)}) collective-permute-start(bf16[352,128]{1,0:T(8,128)(2,1)S(1)} %pack.1.refs_1_), channel_id=1, source_target_pairs={{0,24},{4,28},{8,16},{12,20},{16,8},{20,12},{24,0},{28,4},{1,25},{... | collective-permute-start | bytes 270344 | tf_op jit(solution)/shard_map/ppermute | solution.py:19
  8.6 12.1 %collective-permute-start.5 = (bf16[512,128]{1,0:T(8,128)(2,1)}, bf16[512,128]{1,0:T(8,128)(2,1)S(1)}, u32[]{:S(2)}, u32[]{:S(2)}) collective-permute-start(bf16[512,128]{1,0:T(8,128)(2,1)} %refs_1_.1), channel_id=1, source_target_pairs={{0,1},{1,0},{2,3},{3,2},{4,5},{5,4},{6,7},{7,6},{8,9},{9,8},{10,11... | collective-permute-start | bytes 393224 | tf_op jit(solution)/shard_map/ppermute | solution.py:19
  10.3 10.4 %collective-permute-start.6 = (bf16[512,128]{1,0:T(8,128)(2,1)}, bf16[512,128]{1,0:T(8,128)(2,1)S(1)}, u32[]{:S(2)}, u32[]{:S(2)}) collective-permute-start(bf16[512,128]{1,0:T(8,128)(2,1)} %refs_1_.1), channel_id=1, source_target_pairs={{0,2},{1,3},{2,0},{3,1},{4,6},{5,7},{6,4},{7,5},{8,10},{9,11},{10,... | collective-permute-start | bytes 393224 | tf_op jit(solution)/shard_map/ppermute | solution.py:19
  11.8 8.9 %collective-permute-start.7 = (bf16[512,128]{1,0:T(8,128)(2,1)}, bf16[512,128]{1,0:T(8,128)(2,1)S(1)}, u32[]{:S(2)}, u32[]{:S(2)}) collective-permute-start(bf16[512,128]{1,0:T(8,128)(2,1)} %refs_1_.1), channel_id=1, source_target_pairs={{0,3},{1,2},{2,1},{3,0},{4,7},{5,6},{6,5},{7,4},{8,11},{9,10},{10,... | collective-permute-start | bytes 393224 | tf_op jit(solution)/shard_map/ppermute | solution.py:19
  20.6 2.2 %collective-permute-start.8 = (bf16[256,128]{1,0:T(8,128)(2,1)S(1)}, bf16[256,128]{1,0:T(8,128)(2,1)S(1)}, u32[]{:S(2)}, u32[]{:S(2)}) collective-permute-start(bf16[256,128]{1,0:T(8,128)(2,1)S(1)} %get-tuple-element.13.refs_1_), channel_id=1, source_target_pairs={{0,4},{4,0},{8,12},{12,8},{16,20},{20,16},{24,28},{28,24},{1,5},{5... | collective-permute-start | bytes 196616 | tf_op jit(solution)/shard_map/ppermute | solution.py:19

commit v3 on v2

--- a/solution.py
+++ b/solution.py
@@ -9,7 +9,8 @@
 
 
 SUB = 8
-CHUNK = 512
+AHEAD = 3
+CHUNK = 1024
 
 VMEM = pl.BlockSpec(memory_space=pltpu.VMEM)
 HBM = pl.BlockSpec(memory_space=pltpu.HBM)
@@ -20,7 +21,28 @@
 
 
 def far_steps(n_row):
-    return [2 * i for i in reversed(range(1, n_row // 2))]
+    half = n_row // 2
+    return [half] + [i for i in range(n_row - 2, 0, -2) if i != half]
+
+
+def terms(x):
+    out = []
+    for _ in range(3):
+        out.append(x.astype(jnp.bfloat16).astype(jnp.float32))
+        x = x - out[-1]
+    return out
+
+
+def outer_product(x, y):
+    x, y = terms(x), terms(y)
+    chosen = [(0, 0), (0, 1), (1, 0), (1, 1), (0, 2), (2, 0)]
+    left = [x[i] for i, _ in chosen]
+    right = [y[j] for _, j in chosen]
+    left = jnp.concatenate(left, 0).astype(jnp.bfloat16)
+    right = jnp.concatenate(right, 0).astype(jnp.bfloat16)
+    return lax.dot_general(
+        left, right, (((0,), (0,)), ((), ())), preferred_element_type=jnp.float32
+    )
 
 
 def inverse_factor(tile):
@@ -31,7 +53,7 @@
     sub = lax.broadcasted_iota(jnp.int32, (SUB, n), 0)
 
     def col(x, c):
-        return jnp.broadcast_to(x[:, c : c + 1], (SUB, n))
+        return jnp.take_along_axis(x, jnp.full((SUB, n), c, jnp.int32), axis=1)
 
     def row(x, r):
         return jnp.broadcast_to(x[r : r + 1, :], (SUB, n))
@@ -43,11 +65,10 @@
         here = rows[block]
         cols = [col(here, base + j) for j in range(SUB)]
         here = jnp.where(inside, (lane - base == sub).astype(jnp.float32), here)
-        more = block + 1 < blocks
-        if more:
-            after = rows[block + 1]
-            cols_after = [col(after, base + j) for j in range(SUB)]
-            after = jnp.where(inside, 0.0, after)
+        near = range(block + 1, min(block + 1 + AHEAD, blocks))
+        cols_near = {i: [col(rows[i], base + j) for j in range(SUB)] for i in near}
+        for i in near:
+            rows[i] = jnp.where(inside, 0.0, rows[i])
         pivots = jnp.zeros((SUB, n), jnp.float32)
         scales = jnp.zeros((SUB, n), jnp.float32)
         for k in range(0, SUB, 2):
@@ -60,31 +81,23 @@
             second = row(here, k + 1) - ratio * first
             m1 = jnp.where(sub > k, cols[k], 0.0) * inv_a
             m2 = jnp.where(sub > k + 1, a * cols[k + 1] - b * cols[k], 0.0) * inv_det
-            if more:
-                n1 = cols_after[k] * inv_a
-                n2 = (a * cols_after[k + 1] - b * cols_after[k]) * inv_det
+            n1 = {i: cols_near[i][k] * inv_a for i in near}
+            n2 = {i: (a * cols_near[i][k + 1] - b * cols_near[i][k]) * inv_det for i in near}
             pairs = [(row(cols[j], k), row(cols[j], k + 1)) for j in range(k + 2, SUB)]
             for j, (x1, x2) in zip(range(k + 2, SUB), pairs):
                 x2 = x2 - ratio * x1
                 cols[j] = cols[j] - m1 * x1 - m2 * x2
-                if more:
-                    cols_after[j] = cols_after[j] - n1 * x1 - n2 * x2
+                for i in near:
+                    cols_near[i][j] = cols_near[i][j] - n1[i] * x1 - n2[i] * x2
             here = here - m1 * first - m2 * second
-            if more:
-                after = after - n1 * first - n2 * second
+            for i in near:
+                rows[i] = rows[i] - n1[i] * first - n2[i] * second
             pivots = jnp.where(sub == k, a, jnp.where(sub == k + 1, det * inv_a, pivots))
             scales = jnp.where(sub == k, inv_a, jnp.where(sub == k + 1, a * inv_det, scales))
-        if more:
-            rows[block + 1] = after
-        if block + 2 < blocks:
-            rest = lax.dot_general(
-                here * scales,
-                here,
-                (((0,), (0,)), ((), ())),
-                precision=lax.Precision.HIGHEST,
-                preferred_element_type=jnp.float32,
-            )
-            for i in range(block + 2, blocks):
+        far = range(block + 1 + AHEAD, blocks)
+        if far:
+            rest = outer_product(here * scales, here)
+            for i in far:
                 rows[i] = jnp.where(inside, 0.0, rows[i]) - rest[i * SUB : (i + 1) * SUB]
         out.append(jnp.where(lane <= sub + base, here * lax.rsqrt(pivots), 0.0))
     return out

time: 25 us -> 22.8 us (0.912)
  Pallas kernels: 9.51 us -> 7.29 us
    pallas_call x1, Pallas kernels: 4.54 us -> 2.54 us  [per_device(): pl.pallas_call(functools.partial(inverse_kernel, n_row, half), out_shape=...]
  transfers between devices with their start and end apart: 9 -> 9, of which waited for: 1 -> 1; matrix products, arithmetic and copies ran while one was open for 0% -> 0% of each run, Pallas kernels for 31% -> 24%
where the time goes in v3:
time: 22.8 us; the launch traced here: 22.5 us
  starting transfers between devices  9.84 us (43%)
  Pallas kernels  7.29 us (32%)
  waiting for transfers between devices  3.98 us (17%)
  between operations  0.72 us (3%)
  local copies, waits for them, and re-layouts  0.7 us (3%)
    ppermute x9, starting transfers between devices, exchange(): return lax.ppermute(value, axis, [(i, i ^ step) for i in range(size)])  9.84 us
    ppermute x9, waiting for transfers between devices, exchange(): return lax.ppermute(value, axis, [(i, i ^ step) for i in range(size)])  3.98 us
    pallas_call x2, Pallas kernels, update(): pl.pallas_call(functools.partial(update_kernel, n_col, first_half), out_s...  3.8 us
    pallas_call x1, Pallas kernels, per_device(): pl.pallas_call(functools.partial(inverse_kernel, n_row, half), out_shape=...  2.54 us
    pallas_call x1, Pallas kernels, per_device(): pl.pallas_call(load_kernel, out_shape=[jax.ShapeDtypeStruct(a.shape, a.dt...  0.92 us
    unnamed x2, local copies, waits for them, and re-layouts  0.7 us
  transfers between devices with their start and end apart: 9, of which 1 were waited for; matrix products, arithmetic and copies ran while one was open for 0% of the time, Pallas kernels for 24%

profile of v3, /device:TPU:0, one launch (start us, length us, event | category | flops | bytes accessed | tf_op | source)
XLA Modules:
  0.0 22.5 jit_solution(7046804057602149888)
XLA Ops:
  0.6 0.6 %collective-permute-start.1 = (bf16[512,128]{1,0:T(8,128)(2,1)}, bf16[512,128]{1,0:T(8,128)(2,1)S(1)}, u32[]{:S(2)}, u32[]{:S(2)}) collective-permute-start(bf16[512,128]{1,0:T(8,128)(2,1)} %refs_1_.1), channel_id=1, source_target_pairs={{0,4},{4,0},{8,12},{12,8},{16,20},{20,16},{24,28},{28,24},{1,5},{5... | collective-permute-start | bytes 393224 | tf_op jit(solution)/shard_map/ppermute | solution.py:20
  1.2 0.1 collective-permute-start
  1.3 0.0 copy-start
  1.3 0.7 %copy-done = f32[16,128]{1,0:T(8,128)S(1)} copy-done((f32[16,128]{1,0:T(8,128)S(1)}, f32[16,128]{1,0:T(8,128)}, u32[]{:S(2)}) %copy-start) | copy-done | bytes 8216
  2.0 0.9 %load.1 = (f32[16,128]{1,0:T(8,128)S(1)}, bf16[512,128]{1,0:T(8,128)(2,1)S(1)}) custom-call(f32[16,128]{1,0:T(8,128)S(1)} %copy-done, bf16[512,128]{1,0:T(8,128)(2,1)} %refs_1_.1), custom_call_target="tpu_custom_call" | custom-call | flops 1 | bytes 262144 | tf_op jit(solution)/shard_map/load/pallas_call | solution.py:246
  2.9 0.0 collective-permute-done.refs_1_
  2.9 0.0 collective-permute-done.1.refs_3_
  3.0 3.1 %collective-permute-start.2 = (bf16[352,128]{1,0:T(8,128)(2,1)S(1)}, bf16[352,128]{1,0:T(8,128)(2,1)S(1)}, u32[]{:S(2)}, u32[]{:S(2)}) collective-permute-start(bf16[352,128]{1,0:T(8,128)(2,1)S(1)} %pack.1.refs_1_), channel_id=1, source_target_pairs={{0,8},{4,12},{8,0},{12,4},{16,24},{20,28},{24,16},{28,20},{1,9},{5... | collective-permute-start | bytes 270344 | tf_op jit(solution)/shard_map/ppermute | solution.py:20
  6.0 2.6 %collective-permute-start.3 = (bf16[352,128]{1,0:T(8,128)(2,1)S(1)}, bf16[352,128]{1,0:T(8,128)(2,1)S(1)}, u32[]{:S(2)}, u32[]{:S(2)}) collective-permute-start(bf16[352,128]{1,0:T(8,128)(2,1)S(1)} %pack.1.refs_1_), channel_id=1, source_target_pairs={{0,16},{4,20},{8,24},{12,28},{16,0},{20,4},{24,8},{28,12},{1,17},{... | collective-permute-start | bytes 270344 | tf_op jit(solution)/shard_map/ppermute | solution.py:20
  8.6 0.0 collective-permute-start.4
  8.6 1.7 %collective-permute-start.5 = (bf16[512,128]{1,0:T(8,128)(2,1)}, bf16[512,128]{1,0:T(8,128)(2,1)S(1)}, u32[]{:S(2)}, u32[]{:S(2)}) collective-permute-start(bf16[512,128]{1,0:T(8,128)(2,1)} %refs_1_.1), channel_id=1, source_target_pairs={{0,1},{1,0},{2,3},{3,2},{4,5},{5,4},{6,7},{7,6},{8,9},{9,8},{10,11... | collective-permute-start | bytes 393224 | tf_op jit(solution)/shard_map/ppermute | solution.py:20
  10.3 1.5 %collective-permute-start.6 = (bf16[512,128]{1,0:T(8,128)(2,1)}, bf16[512,128]{1,0:T(8,128)(2,1)S(1)}, u32[]{:S(2)}, u32[]{:S(2)}) collective-permute-start(bf16[512,128]{1,0:T(8,128)(2,1)} %refs_1_.1), channel_id=1, source_target_pairs={{0,2},{1,3},{2,0},{3,1},{4,6},{5,7},{6,4},{7,5},{8,10},{9,11},{10,... | collective-permute-start | bytes 393224 | tf_op jit(solution)/shard_map/ppermute | solution.py:20
  11.8 0.0 collective-permute-done.2.refs_2_
  11.8 0.3 %collective-permute-start.7 = (bf16[512,128]{1,0:T(8,128)(2,1)}, bf16[512,128]{1,0:T(8,128)(2,1)S(1)}, u32[]{:S(2)}, u32[]{:S(2)}) collective-permute-start(bf16[512,128]{1,0:T(8,128)(2,1)} %refs_1_.1), channel_id=1, source_target_pairs={{0,3},{1,2},{2,1},{3,0},{4,7},{5,6},{6,5},{7,4},{8,11},{9,10},{10,... | collective-permute-start | bytes 393224 | tf_op jit(solution)/shard_map/ppermute | solution.py:20
  12.1 4.0 %collective-permute-done.3.refs_3_ = bf16[352,128]{1,0:T(8,128)(2,1)S(1)} collective-permute-done((bf16[352,128]{1,0:T(8,128)(2,1)S(1)}, bf16[352,128]{1,0:T(8,128)(2,1)S(1)}, u32[]{:S(2)}, u32[]{:S(2)}) %collective-permute-start.3) | collective-permute-done | bytes 90144 | tf_op jit(solution)/shard_map/ppermute | solution.py:20
  16.0 0.0 collective-permute-done.4.refs_4_
  16.0 2.5 %inverse.1 = (bf16[256,128]{1,0:T(8,128)(2,1)S(1)}, bf16[128,128]{1,0:T(8,128)(2,1)S(1)}, f32[2048,512]{1,0:T(8,128)S(1)}) custom-call(f32[2048,512]{1,0:T(8,128)} %refs_0_.3, bf16[352,128]{1,0:T(8,128)(2,1)S(1)} %pack.1.refs_1_, bf16[352,128]{1,0:T(8,128)(2,1)S(1)} %collective-permute-done.2.refs_2_, bf16[352,128]{1,0:T(8,128)(2,1)S(1)} %collective-permute-done.3.refs_3_, ...), custom_call_target="tpu_custom_call" | custom-call | flops 4194304 | bytes 98304 | tf_op jit(solution)/shard_map/inverse/pallas_call | solution.py:280
  18.6 0.1 collective-permute-start.8
  18.7 0.0 collective-permute-done.5.refs_4_
  18.7 0.0 collective-permute-done.6.refs_5_
  18.7 0.0 collective-permute-done.7.refs_6_
  18.7 2.0 %update_first.1 = (bf16[512,128]{1,0:T(8,128)(2,1)}, bf16[2048,128]{1,0:T(8,128)(2,1)S(1)}, f32[2048,512]{1,0:T(8,128)}) custom-call(bf16[128,128]{1,0:T(8,128)(2,1)S(1)} %get-tuple-element.12.refs_0_, bf16[256,128]{1,0:T(8,128)(2,1)S(1)} %get-tuple-element.13.refs_1_, f32[2048,512]{1,0:T(8,128)S(1)} %get-tuple-element.14.refs_2_, ...), custom_call_target="tpu_custom_call" | custom-call | flops 134217728 | bytes 4194304 | tf_op jit(solution)/shard_map/update_first/pallas_call | solution.py:303
  20.7 0.0 collective-permute-done.8.refs_1_
  20.7 1.8 %update_second.1 = f32[2048,512]{1,0:T(8,128)} custom-call(bf16[128,128]{1,0:T(8,128)(2,1)S(1)} %get-tuple-element.12.refs_0_, bf16[256,128]{1,0:T(8,128)(2,1)S(1)} %collective-permute-done.8.refs_1_, f32[2048,512]{1,0:T(8,128)S(1)} %get-tuple-element.14.refs_2_, bf16[2048,128]{1,0:T(8,128)(2,1)S(1)} %get-tuple-element.16.refs_3_, ...), custom_call_target="tpu_custom_call", output_to_operand_aliasing={{}: (4, {})} | custom-call | flops 134217728 | bytes 4194304 | tf_op jit(solution)/shard_map/update_second/pallas_call | solution.py:303
  (1 shorter events, 0.0 us)
Async XLA Ops:
  0.6 2.3 %collective-permute-start.1 = (bf16[512,128]{1,0:T(8,128)(2,1)}, bf16[512,128]{1,0:T(8,128)(2,1)S(1)}, u32[]{:S(2)}, u32[]{:S(2)}) collective-permute-start(bf16[512,128]{1,0:T(8,128)(2,1)} %refs_1_.1), channel_id=1, source_target_pairs={{0,4},{4,0},{8,12},{12,8},{16,20},{20,16},{24,28},{28,24},{1,5},{5... | collective-permute-start | bytes 393224 | tf_op jit(solution)/shard_map/ppermute | solution.py:20
  1.2 1.7 %collective-permute-start = (f32[16,128]{1,0:T(8,128)}, f32[16,128]{1,0:T(8,128)S(1)}, u32[]{:S(2)}, u32[]{:S(2)}) collective-permute-start(f32[16,128]{1,0:T(8,128)} %refs_0_.2), channel_id=1, source_target_pairs={{0,4},{4,0},{8,12},{12,8},{16,20},{20,16},{24,28},{28,24},{1,5},{5... | collective-permute-start | bytes 24584 | tf_op jit(solution)/shard_map/ppermute | solution.py:20
  1.3 0.7 %copy-start = (f32[16,128]{1,0:T(8,128)S(1)}, f32[16,128]{1,0:T(8,128)}, u32[]{:S(2)}) copy-start(f32[16,128]{1,0:T(8,128)} %refs_0_.2) | copy-start | bytes 24580
  3.0 8.9 %collective-permute-start.2 = (bf16[352,128]{1,0:T(8,128)(2,1)S(1)}, bf16[352,128]{1,0:T(8,128)(2,1)S(1)}, u32[]{:S(2)}, u32[]{:S(2)}) collective-permute-start(bf16[352,128]{1,0:T(8,128)(2,1)S(1)} %pack.1.refs_1_), channel_id=1, source_target_pairs={{0,8},{4,12},{8,0},{12,4},{16,24},{20,28},{24,16},{28,20},{1,9},{5... | collective-permute-start | bytes 270344 | tf_op jit(solution)/shard_map/ppermute | solution.py:20
  6.0 10.0 %collective-permute-start.3 = (bf16[352,128]{1,0:T(8,128)(2,1)S(1)}, bf16[352,128]{1,0:T(8,128)(2,1)S(1)}, u32[]{:S(2)}, u32[]{:S(2)}) collective-permute-start(bf16[352,128]{1,0:T(8,128)(2,1)S(1)} %pack.1.refs_1_), channel_id=1, source_target_pairs={{0,16},{4,20},{8,24},{12,28},{16,0},{20,4},{24,8},{28,12},{1,17},{... | collective-permute-start | bytes 270344 | tf_op jit(solution)/shard_map/ppermute | solution.py:20
  8.6 7.5 %collective-permute-start.4 = (bf16[352,128]{1,0:T(8,128)(2,1)S(1)}, bf16[352,128]{1,0:T(8,128)(2,1)S(1)}, u32[]{:S(2)}, u32[]{:S(2)}) collective-permute-start(bf16[352,128]{1,0:T(8,128)(2,1)S(1)} %pack.1.refs_1_), channel_id=1, source_target_pairs={{0,24},{4,28},{8,16},{12,20},{16,8},{20,12},{24,0},{28,4},{1,25},{... | collective-permute-start | bytes 270344 | tf_op jit(solution)/shard_map/ppermute | solution.py:20
  8.6 10.1 %collective-permute-start.5 = (bf16[512,128]{1,0:T(8,128)(2,1)}, bf16[512,128]{1,0:T(8,128)(2,1)S(1)}, u32[]{:S(2)}, u32[]{:S(2)}) collective-permute-start(bf16[512,128]{1,0:T(8,128)(2,1)} %refs_1_.1), channel_id=1, source_target_pairs={{0,1},{1,0},{2,3},{3,2},{4,5},{5,4},{6,7},{7,6},{8,9},{9,8},{10,11... | collective-permute-start | bytes 393224 | tf_op jit(solution)/shard_map/ppermute | solution.py:20
  10.3 8.4 %collective-permute-start.6 = (bf16[512,128]{1,0:T(8,128)(2,1)}, bf16[512,128]{1,0:T(8,128)(2,1)S(1)}, u32[]{:S(2)}, u32[]{:S(2)}) collective-permute-start(bf16[512,128]{1,0:T(8,128)(2,1)} %refs_1_.1), channel_id=1, source_target_pairs={{0,2},{1,3},{2,0},{3,1},{4,6},{5,7},{6,4},{7,5},{8,10},{9,11},{10,... | collective-permute-start | bytes 393224 | tf_op jit(solution)/shard_map/ppermute | solution.py:20
  11.8 6.9 %collective-permute-start.7 = (bf16[512,128]{1,0:T(8,128)(2,1)}, bf16[512,128]{1,0:T(8,128)(2,1)S(1)}, u32[]{:S(2)}, u32[]{:S(2)}) collective-permute-start(bf16[512,128]{1,0:T(8,128)(2,1)} %refs_1_.1), channel_id=1, source_target_pairs={{0,3},{1,2},{2,1},{3,0},{4,7},{5,6},{6,5},{7,4},{8,11},{9,10},{10,... | collective-permute-start | bytes 393224 | tf_op jit(solution)/shard_map/ppermute | solution.py:20
  18.6 2.1 %collective-permute-start.8 = (bf16[256,128]{1,0:T(8,128)(2,1)S(1)}, bf16[256,128]{1,0:T(8,128)(2,1)S(1)}, u32[]{:S(2)}, u32[]{:S(2)}) collective-permute-start(bf16[256,128]{1,0:T(8,128)(2,1)S(1)} %get-tuple-element.13.refs_1_), channel_id=1, source_target_pairs={{0,4},{4,0},{8,12},{12,8},{16,20},{20,16},{24,28},{28,24},{1,5},{5... | collective-permute-start | bytes 196616 | tf_op jit(solution)/shard_map/ppermute | solution.py:20

commit v4 on v3

--- a/solution.py
+++ b/solution.py
@@ -10,7 +10,6 @@
 
 SUB = 8
 AHEAD = 3
-CHUNK = 1024
 
 VMEM = pl.BlockSpec(memory_space=pltpu.VMEM)
 HBM = pl.BlockSpec(memory_space=pltpu.HBM)
@@ -43,6 +42,13 @@
     return lax.dot_general(
         left, right, (((0,), (0,)), ((), ())), preferred_element_type=jnp.float32
     )
+
+
+def tree_steps(n_row):
+    steps = [n_row // 4]
+    while steps[-1] > 2:
+        steps.append(steps[-1] // 2)
+    return steps
 
 
 def inverse_factor(tile):
@@ -116,45 +122,39 @@
 
 
 def pack_kernel(half, *refs):
-    tile, tile_beside, *panels, out = refs
-    me = lax.axis_index("row")
-    odd = lax.rem(me, 2) == 1
     if half:
-        panel, panel_beside = panels
-        out[:half, :] = jnp.where(odd, panel_beside[half:, :], panel[:half, :])
+        tile, tile_beside, panel, panel_beside, two, pack = refs
+        odd = lax.rem(lax.axis_index("row"), 2) == 1
+        pack[:half, :] = jnp.where(odd, panel_beside[half:, :], panel[:half, :])
+    else:
+        tile, tile_beside, two = refs
     depth = tile.shape[0]
     for i, ref in enumerate((tile, tile_beside)):
-        rest = ref[...]
-        for term in range(3):
-            start = half + (2 * term + i) * depth
-            value = rest.astype(jnp.bfloat16)
-            out[start : start + depth, :] = value
-            rest = rest - value.astype(jnp.float32)
+        two[i * depth : (i + 1) * depth, :] = ref[...]
+        if half:
+            for term, value in enumerate(terms(ref[...])):
+                start = half + (2 * term + i) * depth
+                pack[start : start + depth, :] = value.astype(jnp.bfloat16)
 
 
 def inverse_kernel(n_row, half, *refs):
-    trailing, *packs = refs[: 1 + n_row // 2]
-    if half:
-        near, out, held, tile, sem = refs[1 + n_row // 2 :]
-    else:
-        out, held, tile, sem = refs[1 + n_row // 2 :]
+    trailing, *packs, out, held, tile, sem = refs
     load = pltpu.make_async_copy(trailing, held, sem)
     load.start()
     me = lax.axis_index("row")
     depth = tile.shape[0] // n_row
     for step, pack in zip(range(0, n_row, 2), packs):
         for i in range(2):
-            terms = []
-            for term in range(3):
-                start = half + (2 * term + i) * depth
-                terms.append(pack[start : start + depth, :].astype(jnp.float32))
+            if pack.dtype == tile.dtype:
+                value = pack[i * depth : (i + 1) * depth, :]
+            else:
+                parts = []
+                for term in range(3):
+                    start = half + (2 * term + i) * depth
+                    parts.append(pack[start : start + depth, :].astype(jnp.float32))
+                value = (parts[0] + parts[1]) + parts[2]
             place = pl.multiple_of((me ^ step ^ i) * depth, depth)
-            tile[pl.ds(place, depth), :] = (terms[0] + terms[1]) + terms[2]
-        if half:
-
-            @pl.when(me - lax.rem(me, 2) == step)
-            def _():
-                near[...] = pack[:half, :]
+            tile[pl.ds(place, depth), :] = value
 
     @pl.when(me >= 0)
     def _():
@@ -171,56 +171,91 @@
     return lax.dot_general(a, b, (((1,), (1,)), ((), ())), preferred_element_type=jnp.float32)
 
 
-def update_kernel(n_col, first_half, *refs):
-    if first_half:
-        inverse, col_rows, held, *pieces = refs[: 3 + n_col]
-        solved, solved_all, updated, new, col_solved, sems, own_sem = refs[3 + n_col :]
+def update_kernel(n_col, first, *refs):
+    early = n_col // 2
+    count = early if first else n_col - early
+    inverse, col_rows, held = refs[:3]
+    pieces, refs = refs[3 : 3 + count], refs[3 + count :]
+    if first:
+        solved, all_rows, cols_near, updated, new, sems, own_sem = refs
     else:
-        inverse, col_rows, held, solved_all, _, updated, new, col_solved, sems, _ = refs
+        early_rows, cols_near, _, updated, new, sems, cols_other, all_rows = refs
     row, col = lax.axis_index("row"), lax.axis_index("col")
     rows_dev, cols_dev = held.shape
     width = cols_dev // 2
+    depth = rows_dev // n_col
     odd = lax.rem(row, 2)
-    lanes = pl.multiple_of((odd if first_half else 1 - odd) * width, width)
+    lanes_near = pl.multiple_of(odd * width, width)
+    lanes_other = pl.multiple_of((1 - odd) * width, width)
     weights = inverse[...]
-    col_solved[...] = product(col_rows[...], weights).astype(col_solved.dtype)
-    if first_half:
-        depth = pieces[0].shape[0]
-        for step in range(n_col):
-            place = pl.ds(pl.multiple_of((col ^ step) * depth, depth), depth)
-            rows = product(pieces[step][...], weights)
-            solved_all[place, :] = rows.astype(solved_all.dtype)
-        own = pl.ds(pl.multiple_of(col * depth, depth), depth)
-        save = pltpu.make_async_copy(solved_all.at[own], solved, own_sem)
+
+    def place_of(step):
+        return pl.ds(pl.multiple_of((col ^ step) * depth, depth), depth)
+
+    def store(step, lanes, slot):
+        return pltpu.make_async_copy(
+            new.at[pl.ds(slot * depth, depth)],
+            updated.at[place_of(step), pl.ds(lanes, width)],
+            sems.at[slot],
+        )
+
+    def block(step, rows, cols, lanes, slot):
+        place = place_of(step)
+        update = product(rows[...], cols[...])
+        ahead = row * rows_dev + (col ^ step) * depth - (col * cols_dev + lanes)
+        row_ids = lax.broadcasted_iota(jnp.int32, (depth, width), 0)
+        col_ids = lax.broadcasted_iota(jnp.int32, (depth, width), 1)
+        old = held[place, pl.ds(lanes, width)]
+        new[pl.ds(slot * depth, depth), :] = old - jnp.where(
+            col_ids - row_ids <= ahead, update, 0.0
+        )
+        store(step, lanes, slot).start()
+
+    cols = cols_near if first else cols_other
+    cols[...] = product(col_rows[...], weights).astype(cols.dtype)
+
+    def solve():
+        for i in range(count):
+            rows = product(pieces[i][...], weights)
+            all_rows[i * depth : (i + 1) * depth, :] = rows.astype(all_rows.dtype)
+
+    def part(i):
+        return pl.ds(pl.multiple_of(i * depth, depth), depth)
+
+    if first:
+        solve()
+        save = pltpu.make_async_copy(all_rows.at[part(0)], solved, own_sem)
         save.start()
-    chunk = min(CHUNK, rows_dev)
-    chunks = rows_dev // chunk
-    ahead = row * rows_dev - (col * cols_dev + lanes)
-
-    def store(i):
-        place = pl.ds(pl.multiple_of(i * chunk, chunk), chunk)
-        return pltpu.make_async_copy(
-            new.at[place], updated.at[place, pl.ds(lanes, width)], sems.at[i]
-        )
-
-    @pl.loop(0, chunks)
-    def _(i):
-        start = pl.multiple_of(i * chunk, chunk)
-        place = pl.ds(start, chunk)
-        update = product(solved_all[place, :], col_solved[...])
-        row_ids = lax.broadcasted_iota(jnp.int32, (chunk, width), 0)
-        col_ids = lax.broadcasted_iota(jnp.int32, (chunk, width), 1)
-        lower = col_ids - row_ids <= ahead + start
-        old = held[place, pl.ds(lanes, width)]
-        new[place, :] = old - jnp.where(lower, update, 0.0)
-        store(i).start()
-
-    @pl.loop(0, chunks)
-    def _(i):
-        store(i).wait()
-
-    if first_half:
+
+        @pl.loop(0, early)
+        def _(i):
+            block(i, all_rows.at[part(i)], cols_near, lanes_near, i)
+
+        @pl.loop(0, early)
+        def _(i):
+            store(i, lanes_near, i).wait()
+
         save.wait()
+    else:
+
+        @pl.loop(0, early)
+        def _(i):
+            block(i, early_rows.at[part(i)], cols_other, lanes_other, i)
+
+        solve()
+
+        @pl.loop(0, count)
+        def _(i):
+            block(early + i, all_rows.at[part(i)], cols_near, lanes_near, n_col + i)
+            block(early + i, all_rows.at[part(i)], cols_other, lanes_other, early + i)
+
+        @pl.loop(0, n_col)
+        def _(i):
+            store(i, lanes_other, i).wait()
+
+        @pl.loop(0, count)
+        def _(i):
+            store(early + i, lanes_near, n_col + i).wait()
 
 
 def column_rows(panel, n_col, cols_dev):
@@ -252,36 +287,49 @@
         cost_estimate=pl.CostEstimate(flops=1, bytes_accessed=4 * depth * width, transcendentals=0),
         compiler_params=pltpu.CompilerParams(vmem_limit_bytes=4 * 1024 * 1024),
         name="load",
-    )(diag_tile, panel)
+    )(
+        pltpu.with_memory_space_constraint(diag_tile, pltpu.HBM),
+        pltpu.with_memory_space_constraint(panel, pltpu.HBM),
+    )
     packed = [tile_near, exchange(diag_tile, "row", n_row, 1)]
+    outs = [jax.ShapeDtypeStruct((2 * diag_tile.shape[0], width), jnp.float32)]
     if direct:
         packed += [panel_near, exchange(panel, "row", n_row, 1)]
+        pack_shape = (half + 6 * diag_tile.shape[0], width)
+        outs.append(jax.ShapeDtypeStruct(pack_shape, panel.dtype))
     pieces.insert(0, panel_near)
-    pack_shape = (half + 6 * diag_tile.shape[0], width)
-    pack = pl.pallas_call(
+    two, *pack = pl.pallas_call(
         functools.partial(pack_kernel, half),
-        out_shape=jax.ShapeDtypeStruct(pack_shape, jnp.bfloat16),
+        out_shape=outs,
         in_specs=[VMEM] * len(packed),
-        out_specs=VMEM,
-        cost_estimate=pl.CostEstimate(flops=1, bytes_accessed=4 * half * width, transcendentals=0),
+        out_specs=[VMEM] * len(outs),
+        cost_estimate=pl.CostEstimate(flops=1, bytes_accessed=4 * depth * width, transcendentals=0),
         compiler_params=pltpu.CompilerParams(vmem_limit_bytes=4 * 1024 * 1024),
         name="pack",
     )(*packed)
-    packs = {0: pack}
+    middle = n_row // 2
+    packs = {0: two}
     for step in far_steps(n_row):
-        packs[step] = exchange(pack, "row", n_row, step)
+        value = pack[0] if direct and step == middle else two
+        packs[step] = exchange(value, "row", n_row, step)
+    row = lax.axis_index("row")
+    if direct:
+        near = jnp.where(row & middle != 0, packs[middle][:half], pack[0][:half])
+        for step in tree_steps(n_row):
+            came = exchange(near, "row", n_row, step)
+            near = jnp.where(row & step != 0, came, near)
+        other = exchange(near, "row", n_row, 1)
+    else:
+        near, other = column_rows(panel, n_col, cols_dev)
     packs = [packs[step] for step in range(0, n_row, 2)]
-    outs = [
-        jax.ShapeDtypeStruct((width, width), jnp.bfloat16),
-        jax.ShapeDtypeStruct(trailing.shape, trailing.dtype),
-    ]
-    if direct:
-        outs = [jax.ShapeDtypeStruct((half, width), panel.dtype)] + outs
-    *near, inverse, held = pl.pallas_call(
+    inverse, held = pl.pallas_call(
         functools.partial(inverse_kernel, n_row, half),
-        out_shape=outs,
+        out_shape=[
+            jax.ShapeDtypeStruct((width, width), jnp.bfloat16),
+            jax.ShapeDtypeStruct(trailing.shape, trailing.dtype),
+        ],
         in_specs=[HBM] + [VMEM] * (n_row // 2),
-        out_specs=[VMEM] * len(outs),
+        out_specs=[VMEM] * 2,
         scratch_shapes=[
             pltpu.VMEM((width, width), jnp.float32),
             pltpu.SemaphoreType.DMA,
@@ -292,44 +340,53 @@
         compiler_params=pltpu.CompilerParams(vmem_limit_bytes=48 * 1024 * 1024),
         name="inverse",
     )(trailing, *packs)
-    if direct:
-        near = near[0]
-        other = exchange(near, "row", n_row, 1)
-    else:
-        near, other = column_rows(panel, n_col, cols_dev)
-    chunks = rows_dev // min(CHUNK, rows_dev)
-
-    def update(first_half, operands, outs, out_specs, aliases):
-        return pl.pallas_call(
-            functools.partial(update_kernel, n_col, first_half),
-            out_shape=outs,
-            in_specs=[VMEM] * (len(operands) - len(aliases)) + [HBM] * len(aliases),
-            out_specs=out_specs,
-            scratch_shapes=[
-                pltpu.VMEM((rows_dev, cols_dev // 2), trailing.dtype),
-                pltpu.VMEM((cols_dev // 2, width), panel.dtype),
-                pltpu.SemaphoreType.DMA((chunks,)),
-                pltpu.SemaphoreType.DMA,
-            ],
-            input_output_aliases=aliases,
-            compiler_params=pltpu.CompilerParams(vmem_limit_bytes=16 * 1024 * 1024),
-            cost_estimate=pl.CostEstimate(
-                flops=rows_dev * cols_dev * width,
-                bytes_accessed=rows_dev * cols_dev * 4,
-                transcendentals=0,
-            ),
-            name="update_first" if first_half else "update_second",
-        )(*operands)
-
+
+    early = n_col // 2
+    late = n_col - early
     slab = jax.ShapeDtypeStruct(trailing.shape, trailing.dtype)
     own = jax.ShapeDtypeStruct(panel.shape, panel.dtype)
-    block = jax.ShapeDtypeStruct((rows_dev, width), panel.dtype)
-    solved, solved_all, updated = update(
-        True, (inverse, near, held, *pieces), (own, block, slab), (HBM, VMEM, HBM), {}
+    early_rows = jax.ShapeDtypeStruct((early * depth, width), panel.dtype)
+    cols_near = jax.ShapeDtypeStruct((cols_dev // 2, width), panel.dtype)
+    params = dict(
+        compiler_params=pltpu.CompilerParams(vmem_limit_bytes=16 * 1024 * 1024),
+        cost_estimate=pl.CostEstimate(
+            flops=rows_dev * cols_dev * width,
+            bytes_accessed=rows_dev * cols_dev * 4,
+            transcendentals=0,
+        ),
     )
-    updated = update(
-        False, (inverse, other, held, solved_all, updated), slab, HBM, {4: 0}
-    )
+
+    def new(blocks):
+        return pltpu.VMEM((blocks * depth, cols_dev // 2), trailing.dtype)
+
+    solved, early_rows, cols_near, updated = pl.pallas_call(
+        functools.partial(update_kernel, n_col, True),
+        out_shape=[own, early_rows, cols_near, slab],
+        in_specs=[VMEM] * (3 + early),
+        out_specs=[HBM, VMEM, VMEM, HBM],
+        scratch_shapes=[
+            new(early),
+            pltpu.SemaphoreType.DMA((early,)),
+            pltpu.SemaphoreType.DMA,
+        ],
+        name="update_first",
+        **params,
+    )(inverse, near, held, *pieces[:early])
+    updated = pl.pallas_call(
+        functools.partial(update_kernel, n_col, False),
+        out_shape=slab,
+        in_specs=[VMEM] * (5 + late) + [HBM],
+        out_specs=HBM,
+        scratch_shapes=[
+            new(n_col + late),
+            pltpu.SemaphoreType.DMA((n_col + late,)),
+            pltpu.VMEM((cols_dev // 2, width), panel.dtype),
+            pltpu.VMEM((late * depth, width), panel.dtype),
+        ],
+        input_output_aliases={5 + late: 0},
+        name="update_second",
+        **params,
+    )(inverse, other, held, *pieces[early:], early_rows, cols_near, updated)
     return solved, updated
 
 

time: 22.8 us -> 32.1 us (1.41)
  waiting for transfers between devices: 3.98 us -> 9.93 us
  starting transfers between devices: 9.84 us -> 13.7 us
  local copies, waits for them, and re-layouts: 0.7 us -> 0 us
    ppermute x9 -> x10, waiting for transfers between devices: 3.98 us -> 9.93 us  [exchange(): return lax.ppermute(value, axis, [(i, i ^ step) for i in range(size)])]
    ppermute x9 -> x10, starting transfers between devices: 9.84 us -> 13.7 us  [exchange(): return lax.ppermute(value, axis, [(i, i ^ step) for i in range(size)])]
    unnamed x2 -> x0, local copies, waits for them, and re-layouts: 0.7 us -> none
  transfers between devices with their start and end apart: 9 -> 10, of which waited for: 1 -> 4; matrix products, arithmetic and copies ran while one was open for 0% -> 0% of each run, Pallas kernels for 24% -> 16%
where the time goes in v4:
time: 32.1 us; the launch traced here: 31.9 us
  starting transfers between devices  13.7 us (43%)
  waiting for transfers between devices  9.93 us (31%)
  Pallas kernels  7.56 us (24%)
  between operations  0.71 us (2%)
    ppermute x10, starting transfers between devices, exchange(): return lax.ppermute(value, axis, [(i, i ^ step) for i in range(size)])  13.7 us
    ppermute x10, waiting for transfers between devices, exchange(): return lax.ppermute(value, axis, [(i, i ^ step) for i in range(size)])  9.93 us
    pallas_call x1, Pallas kernels, per_device(): pl.pallas_call(functools.partial(update_kernel, n_col, False), out_shape=...  2.53 us
    pallas_call x1, Pallas kernels, per_device(): pl.pallas_call(functools.partial(inverse_kernel, n_row, half), out_shape=...  2.52 us
    pallas_call x1, Pallas kernels, per_device(): pl.pallas_call(functools.partial(update_kernel, n_col, True), out_shape=[...  1.54 us
    pallas_call x1, Pallas kernels, per_device(): pl.pallas_call(load_kernel, out_shape=[jax.ShapeDtypeStruct(a.shape, a.dt...  0.94 us
  transfers between devices with their start and end apart: 10, of which 4 were waited for; matrix products, arithmetic and copies ran while one was open for 0% of the time, Pallas kernels for 16%

profile of v4, /device:TPU:0, one launch (start us, length us, event | category | flops | bytes accessed | tf_op | source)
XLA Modules:
  0.0 31.9 jit_solution(17289636146622493356)
XLA Ops:
  0.6 0.6 %collective-permute-start.1 = (bf16[512,128]{1,0:T(8,128)(2,1)}, bf16[512,128]{1,0:T(8,128)(2,1)S(1)}, u32[]{:S(2)}, u32[]{:S(2)}) collective-permute-start(bf16[512,128]{1,0:T(8,128)(2,1)} %refs_1_.1), channel_id=1, source_target_pairs={{0,4},{4,0},{8,12},{12,8},{16,20},{20,16},{24,28},{28,24},{1,5},{5... | collective-permute-start | bytes 393224 | tf_op jit(solution)/shard_map/ppermute | solution.py:19
  1.2 0.1 collective-permute-start
  1.3 0.9 %load.1 = (f32[16,128]{1,0:T(8,128)S(1)}, bf16[512,128]{1,0:T(8,128)(2,1)S(1)}) custom-call(f32[16,128]{1,0:T(8,128)} %refs_0_.2, bf16[512,128]{1,0:T(8,128)(2,1)} %refs_1_.1), custom_call_target="tpu_custom_call" | custom-call | flops 1 | bytes 262144 | tf_op jit(solution)/shard_map/load/pallas_call | solution.py:281
  2.2 0.4 %collective-permute-done.refs_1_ = f32[16,128]{1,0:T(8,128)S(1)} collective-permute-done((f32[16,128]{1,0:T(8,128)}, f32[16,128]{1,0:T(8,128)S(1)}, u32[]{:S(2)}, u32[]{:S(2)}) %collective-permute-start) | collective-permute-done | bytes 8224 | tf_op jit(solution)/shard_map/ppermute | solution.py:19
  2.6 0.0 collective-permute-done.1.refs_3_
  2.6 3.8 %collective-permute-start.3 = (bf16[352,128]{1,0:T(8,128)(2,1)S(1)}, bf16[352,128]{1,0:T(8,128)(2,1)S(1)}, u32[]{:S(2)}, u32[]{:S(2)}) collective-permute-start(bf16[352,128]{1,0:T(8,128)(2,1)S(1)} %get-tuple-element.15), channel_id=1, source_target_pairs={{0,16},{4,20},{8,24},{12,28},{16,0},{20,4},{24,8},{28,12},{1,17},{... | collective-permute-start | bytes 270344 | tf_op jit(solution)/shard_map/ppermute | solution.py:19
  6.4 5.0 %collective-permute-done.3.refs_3_ = bf16[352,128]{1,0:T(8,128)(2,1)S(1)} collective-permute-done((bf16[352,128]{1,0:T(8,128)(2,1)S(1)}, bf16[352,128]{1,0:T(8,128)(2,1)S(1)}, u32[]{:S(2)}, u32[]{:S(2)}) %collective-permute-start.3) | collective-permute-done | bytes 90144 | tf_op jit(solution)/shard_map/ppermute | solution.py:19
  11.5 0.8 %collective-permute-start.5 = (bf16[256,128]{1,0:T(8,128)(2,1)S(1)}, bf16[256,128]{1,0:T(8,128)(2,1)S(1)}, u32[]{:S(2)}, u32[]{:S(2)}) collective-permute-start(bf16[256,128]{1,0:T(8,128)(2,1)S(1)} %slice_select_fusion), channel_id=1, source_target_pairs={{0,8},{4,12},{8,0},{12,4},{16,24},{20,28},{24,16},{28,20},{1,9},{5... | collective-permute-start | bytes 196616 | tf_op jit(solution)/shard_map/ppermute | solution.py:19
  12.3 1.5 %collective-permute-start.6 = (bf16[512,128]{1,0:T(8,128)(2,1)}, bf16[512,128]{1,0:T(8,128)(2,1)S(1)}, u32[]{:S(2)}, u32[]{:S(2)}) collective-permute-start(bf16[512,128]{1,0:T(8,128)(2,1)} %refs_1_.1), channel_id=1, source_target_pairs={{0,1},{1,0},{2,3},{3,2},{4,5},{5,4},{6,7},{7,6},{8,9},{9,8},{10,11... | collective-permute-start | bytes 393224 | tf_op jit(solution)/shard_map/ppermute | solution.py:19
  13.8 1.5 %collective-permute-start.8 = (bf16[512,128]{1,0:T(8,128)(2,1)}, bf16[512,128]{1,0:T(8,128)(2,1)S(1)}, u32[]{:S(2)}, u32[]{:S(2)}) collective-permute-start(bf16[512,128]{1,0:T(8,128)(2,1)} %refs_1_.1), channel_id=1, source_target_pairs={{0,2},{1,3},{2,0},{3,1},{4,6},{5,7},{6,4},{7,5},{8,10},{9,11},{10,... | collective-permute-start | bytes 393224 | tf_op jit(solution)/shard_map/ppermute | solution.py:19
  15.3 0.5 %collective-permute-start.9 = (bf16[512,128]{1,0:T(8,128)(2,1)}, bf16[512,128]{1,0:T(8,128)(2,1)S(1)}, u32[]{:S(2)}, u32[]{:S(2)}) collective-permute-start(bf16[512,128]{1,0:T(8,128)(2,1)} %refs_1_.1), channel_id=1, source_target_pairs={{0,3},{1,2},{2,1},{3,0},{4,7},{5,6},{6,5},{7,4},{8,11},{9,10},{10,... | collective-permute-start | bytes 393224 | tf_op jit(solution)/shard_map/ppermute | solution.py:19
  15.8 0.0 collective-permute-done.5
  15.8 0.1 collective-permute-start.7
  15.9 1.3 %collective-permute-start.2 = (f32[32,128]{1,0:T(8,128)S(1)}, f32[32,128]{1,0:T(8,128)S(1)}, u32[]{:S(2)}, u32[]{:S(2)}) collective-permute-start(f32[32,128]{1,0:T(8,128)S(1)} %get-tuple-element.14.refs_1_), channel_id=1, source_target_pairs={{0,8},{4,12},{8,0},{12,4},{16,24},{20,28},{24,16},{28,20},{1,9},{5... | collective-permute-start | bytes 49160 | tf_op jit(solution)/shard_map/ppermute | solution.py:19
  17.2 2.5 %collective-permute-done.2.refs_2_ = f32[32,128]{1,0:T(8,128)S(1)} collective-permute-done((f32[32,128]{1,0:T(8,128)S(1)}, f32[32,128]{1,0:T(8,128)S(1)}, u32[]{:S(2)}, u32[]{:S(2)}) %collective-permute-start.2) | collective-permute-done | bytes 16416 | tf_op jit(solution)/shard_map/ppermute | solution.py:19
  19.7 3.5 %collective-permute-start.4 = (f32[32,128]{1,0:T(8,128)S(1)}, f32[32,128]{1,0:T(8,128)S(1)}, u32[]{:S(2)}, u32[]{:S(2)}) collective-permute-start(f32[32,128]{1,0:T(8,128)S(1)} %get-tuple-element.14.refs_1_), channel_id=1, source_target_pairs={{0,24},{4,28},{8,16},{12,20},{16,8},{20,12},{24,0},{28,4},{1,25},{... | collective-permute-start | bytes 49160 | tf_op jit(solution)/shard_map/ppermute | solution.py:19
  23.2 2.0 %collective-permute-done.4.refs_4_ = f32[32,128]{1,0:T(8,128)S(1)} collective-permute-done((f32[32,128]{1,0:T(8,128)S(1)}, f32[32,128]{1,0:T(8,128)S(1)}, u32[]{:S(2)}, u32[]{:S(2)}) %collective-permute-start.4) | collective-permute-done | bytes 16416 | tf_op jit(solution)/shard_map/ppermute | solution.py:19
  25.2 2.5 %inverse.1 = (bf16[128,128]{1,0:T(8,128)(2,1)S(1)}, f32[2048,512]{1,0:T(8,128)S(1)}) custom-call(f32[2048,512]{1,0:T(8,128)} %refs_0_.3, f32[32,128]{1,0:T(8,128)S(1)} %get-tuple-element.14.refs_1_, f32[32,128]{1,0:T(8,128)S(1)} %collective-permute-done.2.refs_2_, bf16[352,128]{1,0:T(8,128)(2,1)S(1)} %collective-permute-done.3.refs_3_, ...), custom_call_target="tpu_custom_call" | custom-call | flops 4194304 | bytes 98304 | tf_op jit(solution)/shard_map/inverse/pallas_call | solution.py:325
  27.8 0.0 collective-permute-done.6.refs_4_
  27.8 1.5 %update_first.1 = (bf16[512,128]{1,0:T(8,128)(2,1)}, bf16[1024,128]{1,0:T(8,128)(2,1)S(1)}, bf16[256,128]{1,0:T(8,128)(2,1)S(1)}, f32[2048,512]{1,0:T(8,128)}) custom-call(bf16[128,128]{1,0:T(8,128)(2,1)S(1)} %get-tuple-element.16.refs_0_, bf16[256,128]{1,0:T(8,128)(2,1)S(1)} %broadcast_select_fusion.refs_1_, f32[2048,512]{1,0:T(8,128)S(1)} %get-tuple-element.17.refs_2_, ...), custom_call_target="tpu_custom_call" | custom-call | flops 134217728 | bytes 4194304 | tf_op jit(solution)/shard_map/update_first/pallas_call | solution.py:362
  29.3 0.0 collective-permute-done.8.refs_3_
  29.3 0.0 collective-permute-done.9.refs_4_
  29.4 0.0 collective-permute-done.7.refs_1_
  29.4 2.5 %update_second.1 = f32[2048,512]{1,0:T(8,128)} custom-call(bf16[128,128]{1,0:T(8,128)(2,1)S(1)} %get-tuple-element.16.refs_0_, bf16[256,128]{1,0:T(8,128)(2,1)S(1)} %collective-permute-done.7.refs_1_, f32[2048,512]{1,0:T(8,128)S(1)} %get-tuple-element.17.refs_2_, ...), custom_call_target="tpu_custom_call", output_to_operand_aliasing={{}: (7, {})} | custom-call | flops 134217728 | bytes 4194304 | tf_op jit(solution)/shard_map/update_second/pallas_call | solution.py:375
  (3 shorter events, 0.0 us)
Async XLA Ops:
  0.6 1.9 %collective-permute-start.1 = (bf16[512,128]{1,0:T(8,128)(2,1)}, bf16[512,128]{1,0:T(8,128)(2,1)S(1)}, u32[]{:S(2)}, u32[]{:S(2)}) collective-permute-start(bf16[512,128]{1,0:T(8,128)(2,1)} %refs_1_.1), channel_id=1, source_target_pairs={{0,4},{4,0},{8,12},{12,8},{16,20},{20,16},{24,28},{28,24},{1,5},{5... | collective-permute-start | bytes 393224 | tf_op jit(solution)/shard_map/ppermute | solution.py:19
  1.2 1.4 %collective-permute-start = (f32[16,128]{1,0:T(8,128)}, f32[16,128]{1,0:T(8,128)S(1)}, u32[]{:S(2)}, u32[]{:S(2)}) collective-permute-start(f32[16,128]{1,0:T(8,128)} %refs_0_.2), channel_id=1, source_target_pairs={{0,4},{4,0},{8,12},{12,8},{16,20},{20,16},{24,28},{28,24},{1,5},{5... | collective-permute-start | bytes 24584 | tf_op jit(solution)/shard_map/ppermute | solution.py:19
  2.6 8.9 %collective-permute-start.3 = (bf16[352,128]{1,0:T(8,128)(2,1)S(1)}, bf16[352,128]{1,0:T(8,128)(2,1)S(1)}, u32[]{:S(2)}, u32[]{:S(2)}) collective-permute-start(bf16[352,128]{1,0:T(8,128)(2,1)S(1)} %get-tuple-element.15), channel_id=1, source_target_pairs={{0,16},{4,20},{8,24},{12,28},{16,0},{20,4},{24,8},{28,12},{1,17},{... | collective-permute-start | bytes 270344 | tf_op jit(solution)/shard_map/ppermute | solution.py:19
  11.5 4.3 %collective-permute-start.5 = (bf16[256,128]{1,0:T(8,128)(2,1)S(1)}, bf16[256,128]{1,0:T(8,128)(2,1)S(1)}, u32[]{:S(2)}, u32[]{:S(2)}) collective-permute-start(bf16[256,128]{1,0:T(8,128)(2,1)S(1)} %slice_select_fusion), channel_id=1, source_target_pairs={{0,8},{4,12},{8,0},{12,4},{16,24},{20,28},{24,16},{28,20},{1,9},{5... | collective-permute-start | bytes 196616 | tf_op jit(solution)/shard_map/ppermute | solution.py:19
  12.3 15.5 %collective-permute-start.6 = (bf16[512,128]{1,0:T(8,128)(2,1)}, bf16[512,128]{1,0:T(8,128)(2,1)S(1)}, u32[]{:S(2)}, u32[]{:S(2)}) collective-permute-start(bf16[512,128]{1,0:T(8,128)(2,1)} %refs_1_.1), channel_id=1, source_target_pairs={{0,1},{1,0},{2,3},{3,2},{4,5},{5,4},{6,7},{7,6},{8,9},{9,8},{10,11... | collective-permute-start | bytes 393224 | tf_op jit(solution)/shard_map/ppermute | solution.py:19
  13.8 15.6 %collective-permute-start.8 = (bf16[512,128]{1,0:T(8,128)(2,1)}, bf16[512,128]{1,0:T(8,128)(2,1)S(1)}, u32[]{:S(2)}, u32[]{:S(2)}) collective-permute-start(bf16[512,128]{1,0:T(8,128)(2,1)} %refs_1_.1), channel_id=1, source_target_pairs={{0,2},{1,3},{2,0},{3,1},{4,6},{5,7},{6,4},{7,5},{8,10},{9,11},{10,... | collective-permute-start | bytes 393224 | tf_op jit(solution)/shard_map/ppermute | solution.py:19
  15.3 14.0 %collective-permute-start.9 = (bf16[512,128]{1,0:T(8,128)(2,1)}, bf16[512,128]{1,0:T(8,128)(2,1)S(1)}, u32[]{:S(2)}, u32[]{:S(2)}) collective-permute-start(bf16[512,128]{1,0:T(8,128)(2,1)} %refs_1_.1), channel_id=1, source_target_pairs={{0,3},{1,2},{2,1},{3,0},{4,7},{5,6},{6,5},{7,4},{8,11},{9,10},{10,... | collective-permute-start | bytes 393224 | tf_op jit(solution)/shard_map/ppermute | solution.py:19
  15.8 13.5 %collective-permute-start.7 = (bf16[256,128]{1,0:T(8,128)(2,1)S(1)}, bf16[256,128]{1,0:T(8,128)(2,1)S(1)}, u32[]{:S(2)}, u32[]{:S(2)}) collective-permute-start(bf16[256,128]{1,0:T(8,128)(2,1)S(1)} %broadcast_select_fusion.refs_1_), channel_id=1, source_target_pairs={{0,4},{4,0},{8,12},{12,8},{16,20},{20,16},{24,28},{28,24},{1,5},{5... | collective-permute-start | bytes 196616 | tf_op jit(solution)/shard_map/ppermute | solution.py:19
  15.9 3.8 %collective-permute-start.2 = (f32[32,128]{1,0:T(8,128)S(1)}, f32[32,128]{1,0:T(8,128)S(1)}, u32[]{:S(2)}, u32[]{:S(2)}) collective-permute-start(f32[32,128]{1,0:T(8,128)S(1)} %get-tuple-element.14.refs_1_), channel_id=1, source_target_pairs={{0,8},{4,12},{8,0},{12,4},{16,24},{20,28},{24,16},{28,20},{1,9},{5... | collective-permute-start | bytes 49160 | tf_op jit(solution)/shard_map/ppermute | solution.py:19
  19.7 5.5 %collective-permute-start.4 = (f32[32,128]{1,0:T(8,128)S(1)}, f32[32,128]{1,0:T(8,128)S(1)}, u32[]{:S(2)}, u32[]{:S(2)}) collective-permute-start(f32[32,128]{1,0:T(8,128)S(1)} %get-tuple-element.14.refs_1_), channel_id=1, source_target_pairs={{0,24},{4,28},{8,16},{12,20},{16,8},{20,12},{24,0},{28,4},{1,25},{... | collective-permute-start | bytes 49160 | tf_op jit(solution)/shard_map/ppermute | solution.py:19

commit v5 on v4

--- a/solution.py
+++ b/solution.py
@@ -177,9 +177,9 @@
     inverse, col_rows, held = refs[:3]
     pieces, refs = refs[3 : 3 + count], refs[3 + count :]
     if first:
-        solved, all_rows, cols_near, updated, new, sems, own_sem = refs
+        solved, rows_early, cols_near, left, own_sem = refs
     else:
-        early_rows, cols_near, _, updated, new, sems, cols_other, all_rows = refs
+        rows_early, cols_near, left, updated, new, sems, cols_other, rows_late = refs
     row, col = lax.axis_index("row"), lax.axis_index("col")
     rows_dev, cols_dev = held.shape
     width = cols_dev // 2
@@ -189,73 +189,60 @@
     lanes_other = pl.multiple_of((1 - odd) * width, width)
     weights = inverse[...]
 
-    def place_of(step):
-        return pl.ds(pl.multiple_of((col ^ step) * depth, depth), depth)
-
-    def store(step, lanes, slot):
-        return pltpu.make_async_copy(
-            new.at[pl.ds(slot * depth, depth)],
-            updated.at[place_of(step), pl.ds(lanes, width)],
-            sems.at[slot],
-        )
-
-    def block(step, rows, cols, lanes, slot):
-        place = place_of(step)
-        update = product(rows[...], cols[...])
-        ahead = row * rows_dev + (col ^ step) * depth - (col * cols_dev + lanes)
+    def part(i):
+        return pl.ds(pl.multiple_of(i * depth, depth), depth)
+
+    def solve(out):
+        for i in range(count):
+            out[part(i), :] = product(pieces[i][...], weights).astype(out.dtype)
+
+    def block(step, rows, cols, lanes):
+        start = pl.multiple_of((col ^ step) * depth, depth)
+        update = jnp.dot(rows[...], cols[...], preferred_element_type=jnp.float32)
+        ahead = row * rows_dev + start - (col * cols_dev + lanes)
         row_ids = lax.broadcasted_iota(jnp.int32, (depth, width), 0)
         col_ids = lax.broadcasted_iota(jnp.int32, (depth, width), 1)
-        old = held[place, pl.ds(lanes, width)]
-        new[pl.ds(slot * depth, depth), :] = old - jnp.where(
-            col_ids - row_ids <= ahead, update, 0.0
-        )
-        store(step, lanes, slot).start()
-
-    cols = cols_near if first else cols_other
-    cols[...] = product(col_rows[...], weights).astype(cols.dtype)
-
-    def solve():
-        for i in range(count):
-            rows = product(pieces[i][...], weights)
-            all_rows[i * depth : (i + 1) * depth, :] = rows.astype(all_rows.dtype)
-
-    def part(i):
-        return pl.ds(pl.multiple_of(i * depth, depth), depth)
+        old = held[pl.ds(start, depth), pl.ds(lanes, width)]
+        return old - jnp.where(col_ids - row_ids <= ahead, update, 0.0)
+
+    def store(step):
+        place = pl.ds(pl.multiple_of((col ^ step) * depth, depth), depth)
+        return pltpu.make_async_copy(new.at[part(step)], updated.at[place], sems.at[step])
 
     if first:
-        solve()
-        save = pltpu.make_async_copy(all_rows.at[part(0)], solved, own_sem)
+        cols_near[...] = product(weights, col_rows[...]).astype(cols_near.dtype)
+        solve(rows_early)
+        save = pltpu.make_async_copy(rows_early.at[part(0)], solved, own_sem)
         save.start()
 
         @pl.loop(0, early)
         def _(i):
-            block(i, all_rows.at[part(i)], cols_near, lanes_near, i)
+            left[part(i), :] = block(i, rows_early.at[part(i)], cols_near, lanes_near)
+
+        save.wait()
+    else:
+        cols_other[...] = product(weights, col_rows[...]).astype(cols_other.dtype)
 
         @pl.loop(0, early)
         def _(i):
-            store(i, lanes_near, i).wait()
-
-        save.wait()
-    else:
-
-        @pl.loop(0, early)
-        def _(i):
-            block(i, early_rows.at[part(i)], cols_other, lanes_other, i)
-
-        solve()
+            new[part(i), pl.ds(lanes_near, width)] = left[part(i), :]
+            new[part(i), pl.ds(lanes_other, width)] = block(
+                i, rows_early.at[part(i)], cols_other, lanes_other
+            )
+            store(i).start()
+
+        solve(rows_late)
 
         @pl.loop(0, count)
         def _(i):
-            block(early + i, all_rows.at[part(i)], cols_near, lanes_near, n_col + i)
-            block(early + i, all_rows.at[part(i)], cols_other, lanes_other, early + i)
+            rows = rows_late.at[part(i)]
+            for cols, lanes in ((cols_near, lanes_near), (cols_other, lanes_other)):
+                new[part(early + i), pl.ds(lanes, width)] = block(early + i, rows, cols, lanes)
+            store(early + i).start()
 
         @pl.loop(0, n_col)
         def _(i):
-            store(i, lanes_other, i).wait()
-
-        @pl.loop(0, count)
-        def _(i):
-            store(early + i, lanes_near, n_col + i).wait()
+            store(i).wait()
 
 
 def column_rows(panel, n_col, cols_dev):
@@ -346,7 +333,8 @@
     slab = jax.ShapeDtypeStruct(trailing.shape, trailing.dtype)
     own = jax.ShapeDtypeStruct(panel.shape, panel.dtype)
     early_rows = jax.ShapeDtypeStruct((early * depth, width), panel.dtype)
-    cols_near = jax.ShapeDtypeStruct((cols_dev // 2, width), panel.dtype)
+    cols_near = jax.ShapeDtypeStruct((width, cols_dev // 2), panel.dtype)
+    left = jax.ShapeDtypeStruct((early * depth, cols_dev // 2), trailing.dtype)
     params = dict(
         compiler_params=pltpu.CompilerParams(vmem_limit_bytes=16 * 1024 * 1024),
         cost_estimate=pl.CostEstimate(
@@ -355,38 +343,29 @@
             transcendentals=0,
         ),
     )
-
-    def new(blocks):
-        return pltpu.VMEM((blocks * depth, cols_dev // 2), trailing.dtype)
-
-    solved, early_rows, cols_near, updated = pl.pallas_call(
+    solved, early_rows, cols_near, left = pl.pallas_call(
         functools.partial(update_kernel, n_col, True),
-        out_shape=[own, early_rows, cols_near, slab],
+        out_shape=[own, early_rows, cols_near, left],
         in_specs=[VMEM] * (3 + early),
-        out_specs=[HBM, VMEM, VMEM, HBM],
-        scratch_shapes=[
-            new(early),
-            pltpu.SemaphoreType.DMA((early,)),
-            pltpu.SemaphoreType.DMA,
-        ],
+        out_specs=[HBM, VMEM, VMEM, VMEM],
+        scratch_shapes=[pltpu.SemaphoreType.DMA],
         name="update_first",
         **params,
     )(inverse, near, held, *pieces[:early])
     updated = pl.pallas_call(
         functools.partial(update_kernel, n_col, False),
         out_shape=slab,
-        in_specs=[VMEM] * (5 + late) + [HBM],
+        in_specs=[VMEM] * (6 + late),
         out_specs=HBM,
         scratch_shapes=[
-            new(n_col + late),
-            pltpu.SemaphoreType.DMA((n_col + late,)),
-            pltpu.VMEM((cols_dev // 2, width), panel.dtype),
+            pltpu.VMEM(trailing.shape, trailing.dtype),
+            pltpu.SemaphoreType.DMA((n_col,)),
+            pltpu.VMEM((width, cols_dev // 2), panel.dtype),
             pltpu.VMEM((late * depth, width), panel.dtype),
         ],
-        input_output_aliases={5 + late: 0},
         name="update_second",
         **params,
-    )(inverse, other, held, *pieces[early:], early_rows, cols_near, updated)
+    )(inverse, other, held, *pieces[early:], early_rows, cols_near, left)
     return solved, updated
 
 

time: 32.1 us -> 31.5 us (0.981)
  Pallas kernels: 7.56 us -> 6.89 us
    pallas_call x1, Pallas kernels: 1.54 us -> 0.92 us  [per_device(): pl.pallas_call(functools.partial(update_kernel, n_col, True), out_shape=[...]
  transfers between devices with their start and end apart: 10 -> 10, of which waited for: 4 -> 4; matrix products, arithmetic and copies ran while one was open for 0% -> 0% of each run, Pallas kernels for 16% -> 14%
where the time goes in v5:
time: 31.5 us; the launch traced here: 31.2 us
  starting transfers between devices  13.7 us (43%)
  waiting for transfers between devices  9.93 us (32%)
  Pallas kernels  6.89 us (22%)
  between operations  0.71 us (2%)
    ppermute x10, starting transfers between devices, exchange(): return lax.ppermute(value, axis, [(i, i ^ step) for i in range(size)])  13.7 us
    ppermute x10, waiting for transfers between devices, exchange(): return lax.ppermute(value, axis, [(i, i ^ step) for i in range(size)])  9.93 us
    pallas_call x1, Pallas kernels, per_device(): pl.pallas_call(functools.partial(inverse_kernel, n_row, half), out_shape=...  2.52 us
    pallas_call x1, Pallas kernels, per_device(): pl.pallas_call(functools.partial(update_kernel, n_col, False), out_shape=...  2.49 us
    pallas_call x1, Pallas kernels, per_device(): pl.pallas_call(load_kernel, out_shape=[jax.ShapeDtypeStruct(a.shape, a.dt...  0.94 us
    pallas_call x1, Pallas kernels, per_device(): pl.pallas_call(functools.partial(update_kernel, n_col, True), out_shape=[...  0.92 us
  transfers between devices with their start and end apart: 10, of which 4 were waited for; matrix products, arithmetic and copies ran while one was open for 0% of the time, Pallas kernels for 14%

profile of v5, /device:TPU:0, one launch (start us, length us, event | category | flops | bytes accessed | tf_op | source)
XLA Modules:
  0.0 31.2 jit_solution(5927937600483645903)
XLA Ops:
  0.6 0.6 %collective-permute-start.1 = (bf16[512,128]{1,0:T(8,128)(2,1)}, bf16[512,128]{1,0:T(8,128)(2,1)S(1)}, u32[]{:S(2)}, u32[]{:S(2)}) collective-permute-start(bf16[512,128]{1,0:T(8,128)(2,1)} %refs_1_.1), channel_id=1, source_target_pairs={{0,4},{4,0},{8,12},{12,8},{16,20},{20,16},{24,28},{28,24},{1,5},{5... | collective-permute-start | bytes 393224 | tf_op jit(solution)/shard_map/ppermute | solution.py:19
  1.2 0.1 collective-permute-start
  1.3 0.9 %load.1 = (f32[16,128]{1,0:T(8,128)S(1)}, bf16[512,128]{1,0:T(8,128)(2,1)S(1)}) custom-call(f32[16,128]{1,0:T(8,128)} %refs_0_.2, bf16[512,128]{1,0:T(8,128)(2,1)} %refs_1_.1), custom_call_target="tpu_custom_call" | custom-call | flops 1 | bytes 262144 | tf_op jit(solution)/shard_map/load/pallas_call | solution.py:268
  2.2 0.4 %collective-permute-done.refs_1_ = f32[16,128]{1,0:T(8,128)S(1)} collective-permute-done((f32[16,128]{1,0:T(8,128)}, f32[16,128]{1,0:T(8,128)S(1)}, u32[]{:S(2)}, u32[]{:S(2)}) %collective-permute-start) | collective-permute-done | bytes 8224 | tf_op jit(solution)/shard_map/ppermute | solution.py:19
  2.6 0.0 collective-permute-done.1.refs_3_
  2.6 3.8 %collective-permute-start.3 = (bf16[352,128]{1,0:T(8,128)(2,1)S(1)}, bf16[352,128]{1,0:T(8,128)(2,1)S(1)}, u32[]{:S(2)}, u32[]{:S(2)}) collective-permute-start(bf16[352,128]{1,0:T(8,128)(2,1)S(1)} %get-tuple-element.15), channel_id=1, source_target_pairs={{0,16},{4,20},{8,24},{12,28},{16,0},{20,4},{24,8},{28,12},{1,17},{... | collective-permute-start | bytes 270344 | tf_op jit(solution)/shard_map/ppermute | solution.py:19
  6.4 5.0 %collective-permute-done.3.refs_3_ = bf16[352,128]{1,0:T(8,128)(2,1)S(1)} collective-permute-done((bf16[352,128]{1,0:T(8,128)(2,1)S(1)}, bf16[352,128]{1,0:T(8,128)(2,1)S(1)}, u32[]{:S(2)}, u32[]{:S(2)}) %collective-permute-start.3) | collective-permute-done | bytes 90144 | tf_op jit(solution)/shard_map/ppermute | solution.py:19
  11.5 0.8 %collective-permute-start.5 = (bf16[256,128]{1,0:T(8,128)(2,1)S(1)}, bf16[256,128]{1,0:T(8,128)(2,1)S(1)}, u32[]{:S(2)}, u32[]{:S(2)}) collective-permute-start(bf16[256,128]{1,0:T(8,128)(2,1)S(1)} %slice_select_fusion), channel_id=1, source_target_pairs={{0,8},{4,12},{8,0},{12,4},{16,24},{20,28},{24,16},{28,20},{1,9},{5... | collective-permute-start | bytes 196616 | tf_op jit(solution)/shard_map/ppermute | solution.py:19
  12.3 1.5 %collective-permute-start.6 = (bf16[512,128]{1,0:T(8,128)(2,1)}, bf16[512,128]{1,0:T(8,128)(2,1)S(1)}, u32[]{:S(2)}, u32[]{:S(2)}) collective-permute-start(bf16[512,128]{1,0:T(8,128)(2,1)} %refs_1_.1), channel_id=1, source_target_pairs={{0,1},{1,0},{2,3},{3,2},{4,5},{5,4},{6,7},{7,6},{8,9},{9,8},{10,11... | collective-permute-start | bytes 393224 | tf_op jit(solution)/shard_map/ppermute | solution.py:19
  13.8 1.5 %collective-permute-start.8 = (bf16[512,128]{1,0:T(8,128)(2,1)}, bf16[512,128]{1,0:T(8,128)(2,1)S(1)}, u32[]{:S(2)}, u32[]{:S(2)}) collective-permute-start(bf16[512,128]{1,0:T(8,128)(2,1)} %refs_1_.1), channel_id=1, source_target_pairs={{0,2},{1,3},{2,0},{3,1},{4,6},{5,7},{6,4},{7,5},{8,10},{9,11},{10,... | collective-permute-start | bytes 393224 | tf_op jit(solution)/shard_map/ppermute | solution.py:19
  15.3 0.5 %collective-permute-start.9 = (bf16[512,128]{1,0:T(8,128)(2,1)}, bf16[512,128]{1,0:T(8,128)(2,1)S(1)}, u32[]{:S(2)}, u32[]{:S(2)}) collective-permute-start(bf16[512,128]{1,0:T(8,128)(2,1)} %refs_1_.1), channel_id=1, source_target_pairs={{0,3},{1,2},{2,1},{3,0},{4,7},{5,6},{6,5},{7,4},{8,11},{9,10},{10,... | collective-permute-start | bytes 393224 | tf_op jit(solution)/shard_map/ppermute | solution.py:19
  15.8 0.0 collective-permute-done.5
  15.8 0.1 collective-permute-start.7
  15.9 1.3 %collective-permute-start.2 = (f32[32,128]{1,0:T(8,128)S(1)}, f32[32,128]{1,0:T(8,128)S(1)}, u32[]{:S(2)}, u32[]{:S(2)}) collective-permute-start(f32[32,128]{1,0:T(8,128)S(1)} %get-tuple-element.14.refs_1_), channel_id=1, source_target_pairs={{0,8},{4,12},{8,0},{12,4},{16,24},{20,28},{24,16},{28,20},{1,9},{5... | collective-permute-start | bytes 49160 | tf_op jit(solution)/shard_map/ppermute | solution.py:19
  17.2 2.5 %collective-permute-done.2.refs_2_ = f32[32,128]{1,0:T(8,128)S(1)} collective-permute-done((f32[32,128]{1,0:T(8,128)S(1)}, f32[32,128]{1,0:T(8,128)S(1)}, u32[]{:S(2)}, u32[]{:S(2)}) %collective-permute-start.2) | collective-permute-done | bytes 16416 | tf_op jit(solution)/shard_map/ppermute | solution.py:19
  19.7 3.5 %collective-permute-start.4 = (f32[32,128]{1,0:T(8,128)S(1)}, f32[32,128]{1,0:T(8,128)S(1)}, u32[]{:S(2)}, u32[]{:S(2)}) collective-permute-start(f32[32,128]{1,0:T(8,128)S(1)} %get-tuple-element.14.refs_1_), channel_id=1, source_target_pairs={{0,24},{4,28},{8,16},{12,20},{16,8},{20,12},{24,0},{28,4},{1,25},{... | collective-permute-start | bytes 49160 | tf_op jit(solution)/shard_map/ppermute | solution.py:19
  23.2 2.0 %collective-permute-done.4.refs_4_ = f32[32,128]{1,0:T(8,128)S(1)} collective-permute-done((f32[32,128]{1,0:T(8,128)S(1)}, f32[32,128]{1,0:T(8,128)S(1)}, u32[]{:S(2)}, u32[]{:S(2)}) %collective-permute-start.4) | collective-permute-done | bytes 16416 | tf_op jit(solution)/shard_map/ppermute | solution.py:19
  25.2 2.5 %inverse.1 = (bf16[128,128]{1,0:T(8,128)(2,1)S(1)}, f32[2048,512]{1,0:T(8,128)S(1)}) custom-call(f32[2048,512]{1,0:T(8,128)} %refs_0_.3, f32[32,128]{1,0:T(8,128)S(1)} %get-tuple-element.14.refs_1_, f32[32,128]{1,0:T(8,128)S(1)} %collective-permute-done.2.refs_2_, bf16[352,128]{1,0:T(8,128)(2,1)S(1)} %collective-permute-done.3.refs_3_, ...), custom_call_target="tpu_custom_call" | custom-call | flops 4194304 | bytes 98304 | tf_op jit(solution)/shard_map/inverse/pallas_call | solution.py:312
  27.8 0.0 collective-permute-done.6.refs_4_
  27.8 0.9 %update_first.1 = (bf16[512,128]{1,0:T(8,128)(2,1)}, bf16[1024,128]{1,0:T(8,128)(2,1)S(1)}, bf16[128,256]{1,0:T(8,128)(2,1)S(1)}, f32[1024,256]{1,0:T(8,128)S(1)}) custom-call(bf16[128,128]{1,0:T(8,128)(2,1)S(1)} %get-tuple-element.16.refs_0_, bf16[256,128]{1,0:T(8,128)(2,1)S(1)} %broadcast_select_fusion.refs_1_, f32[2048,512]{1,0:T(8,128)S(1)} %get-tuple-element.17.refs_2_, ...), custom_call_target="tpu_custom_call" | custom-call | flops 134217728 | bytes 4194304 | tf_op jit(solution)/shard_map/update_first/pallas_call | solution.py:346
  28.7 0.0 collective-permute-done.8.refs_3_
  28.7 0.0 collective-permute-done.9.refs_4_
  28.7 0.0 collective-permute-done.7.refs_1_
  28.7 2.5 %update_second.1 = f32[2048,512]{1,0:T(8,128)} custom-call(bf16[128,128]{1,0:T(8,128)(2,1)S(1)} %get-tuple-element.16.refs_0_, bf16[256,128]{1,0:T(8,128)(2,1)S(1)} %collective-permute-done.7.refs_1_, f32[2048,512]{1,0:T(8,128)S(1)} %get-tuple-element.17.refs_2_, bf16[512,128]{1,0:T(8,128)(2,1)S(1)} %collective-permute-done.8.refs_3_, ...), custom_call_target="tpu_custom_call" | custom-call | flops 134217728 | bytes 4194304 | tf_op jit(solution)/shard_map/update_second/pallas_call | solution.py:355
  (3 shorter events, 0.0 us)
Async XLA Ops:
  0.6 1.9 %collective-permute-start.1 = (bf16[512,128]{1,0:T(8,128)(2,1)}, bf16[512,128]{1,0:T(8,128)(2,1)S(1)}, u32[]{:S(2)}, u32[]{:S(2)}) collective-permute-start(bf16[512,128]{1,0:T(8,128)(2,1)} %refs_1_.1), channel_id=1, source_target_pairs={{0,4},{4,0},{8,12},{12,8},{16,20},{20,16},{24,28},{28,24},{1,5},{5... | collective-permute-start | bytes 393224 | tf_op jit(solution)/shard_map/ppermute | solution.py:19
  1.2 1.4 %collective-permute-start = (f32[16,128]{1,0:T(8,128)}, f32[16,128]{1,0:T(8,128)S(1)}, u32[]{:S(2)}, u32[]{:S(2)}) collective-permute-start(f32[16,128]{1,0:T(8,128)} %refs_0_.2), channel_id=1, source_target_pairs={{0,4},{4,0},{8,12},{12,8},{16,20},{20,16},{24,28},{28,24},{1,5},{5... | collective-permute-start | bytes 24584 | tf_op jit(solution)/shard_map/ppermute | solution.py:19
  2.6 8.9 %collective-permute-start.3 = (bf16[352,128]{1,0:T(8,128)(2,1)S(1)}, bf16[352,128]{1,0:T(8,128)(2,1)S(1)}, u32[]{:S(2)}, u32[]{:S(2)}) collective-permute-start(bf16[352,128]{1,0:T(8,128)(2,1)S(1)} %get-tuple-element.15), channel_id=1, source_target_pairs={{0,16},{4,20},{8,24},{12,28},{16,0},{20,4},{24,8},{28,12},{1,17},{... | collective-permute-start | bytes 270344 | tf_op jit(solution)/shard_map/ppermute | solution.py:19
  11.5 4.3 %collective-permute-start.5 = (bf16[256,128]{1,0:T(8,128)(2,1)S(1)}, bf16[256,128]{1,0:T(8,128)(2,1)S(1)}, u32[]{:S(2)}, u32[]{:S(2)}) collective-permute-start(bf16[256,128]{1,0:T(8,128)(2,1)S(1)} %slice_select_fusion), channel_id=1, source_target_pairs={{0,8},{4,12},{8,0},{12,4},{16,24},{20,28},{24,16},{28,20},{1,9},{5... | collective-permute-start | bytes 196616 | tf_op jit(solution)/shard_map/ppermute | solution.py:19
  12.3 15.5 %collective-permute-start.6 = (bf16[512,128]{1,0:T(8,128)(2,1)}, bf16[512,128]{1,0:T(8,128)(2,1)S(1)}, u32[]{:S(2)}, u32[]{:S(2)}) collective-permute-start(bf16[512,128]{1,0:T(8,128)(2,1)} %refs_1_.1), channel_id=1, source_target_pairs={{0,1},{1,0},{2,3},{3,2},{4,5},{5,4},{6,7},{7,6},{8,9},{9,8},{10,11... | collective-permute-start | bytes 393224 | tf_op jit(solution)/shard_map/ppermute | solution.py:19
  13.8 14.9 %collective-permute-start.8 = (bf16[512,128]{1,0:T(8,128)(2,1)}, bf16[512,128]{1,0:T(8,128)(2,1)S(1)}, u32[]{:S(2)}, u32[]{:S(2)}) collective-permute-start(bf16[512,128]{1,0:T(8,128)(2,1)} %refs_1_.1), channel_id=1, source_target_pairs={{0,2},{1,3},{2,0},{3,1},{4,6},{5,7},{6,4},{7,5},{8,10},{9,11},{10,... | collective-permute-start | bytes 393224 | tf_op jit(solution)/shard_map/ppermute | solution.py:19
  15.3 13.4 %collective-permute-start.9 = (bf16[512,128]{1,0:T(8,128)(2,1)}, bf16[512,128]{1,0:T(8,128)(2,1)S(1)}, u32[]{:S(2)}, u32[]{:S(2)}) collective-permute-start(bf16[512,128]{1,0:T(8,128)(2,1)} %refs_1_.1), channel_id=1, source_target_pairs={{0,3},{1,2},{2,1},{3,0},{4,7},{5,6},{6,5},{7,4},{8,11},{9,10},{10,... | collective-permute-start | bytes 393224 | tf_op jit(solution)/shard_map/ppermute | solution.py:19
  15.8 12.9 %collective-permute-start.7 = (bf16[256,128]{1,0:T(8,128)(2,1)S(1)}, bf16[256,128]{1,0:T(8,128)(2,1)S(1)}, u32[]{:S(2)}, u32[]{:S(2)}) collective-permute-start(bf16[256,128]{1,0:T(8,128)(2,1)S(1)} %broadcast_select_fusion.refs_1_), channel_id=1, source_target_pairs={{0,4},{4,0},{8,12},{12,8},{16,20},{20,16},{24,28},{28,24},{1,5},{5... | collective-permute-start | bytes 196616 | tf_op jit(solution)/shard_map/ppermute | solution.py:19
  15.9 3.8 %collective-permute-start.2 = (f32[32,128]{1,0:T(8,128)S(1)}, f32[32,128]{1,0:T(8,128)S(1)}, u32[]{:S(2)}, u32[]{:S(2)}) collective-permute-start(f32[32,128]{1,0:T(8,128)S(1)} %get-tuple-element.14.refs_1_), channel_id=1, source_target_pairs={{0,8},{4,12},{8,0},{12,4},{16,24},{20,28},{24,16},{28,20},{1,9},{5... | collective-permute-start | bytes 49160 | tf_op jit(solution)/shard_map/ppermute | solution.py:19
  19.7 5.5 %collective-permute-start.4 = (f32[32,128]{1,0:T(8,128)S(1)}, f32[32,128]{1,0:T(8,128)S(1)}, u32[]{:S(2)}, u32[]{:S(2)}) collective-permute-start(f32[32,128]{1,0:T(8,128)S(1)} %get-tuple-element.14.refs_1_), channel_id=1, source_target_pairs={{0,24},{4,28},{8,16},{12,20},{16,8},{20,12},{24,0},{28,4},{1,25},{... | collective-permute-start | bytes 49160 | tf_op jit(solution)/shard_map/ppermute | solution.py:19

commit v6 on v5

--- a/solution.py
+++ b/solution.py
@@ -262,9 +262,6 @@
     depth, width = panel.shape
     direct = depth == cols_dev and n_col * cols_dev <= rows_dev
     half = depth // 2 if direct else 0
-    pieces = []
-    for step in range(1, n_col):
-        pieces.append(exchange(panel, "col", n_col, step))
     tile_near, panel_near = pl.pallas_call(
         load_kernel,
         out_shape=[jax.ShapeDtypeStruct(a.shape, a.dtype) for a in (diag_tile, panel)],
@@ -284,7 +281,9 @@
         packed += [panel_near, exchange(panel, "row", n_row, 1)]
         pack_shape = (half + 6 * diag_tile.shape[0], width)
         outs.append(jax.ShapeDtypeStruct(pack_shape, panel.dtype))
-    pieces.insert(0, panel_near)
+    pieces = [panel_near]
+    for step in range(1, n_col):
+        pieces.append(exchange(panel_near, "col", n_col, step))
     two, *pack = pl.pallas_call(
         functools.partial(pack_kernel, half),
         out_shape=outs,

time: 31.5 us -> 31.5 us (level)
  no operation moved by 1% of the time
where the time goes in v6:
time: 31.5 us; the launch traced here: 31.2 us
  starting transfers between devices  13.7 us (43%)
  waiting for transfers between devices  9.93 us (32%)
  Pallas kernels  6.89 us (22%)
  between operations  0.71 us (2%)
    ppermute x10, starting transfers between devices, exchange(): return lax.ppermute(value, axis, [(i, i ^ step) for i in range(size)])  13.7 us
    ppermute x10, waiting for transfers between devices, exchange(): return lax.ppermute(value, axis, [(i, i ^ step) for i in range(size)])  9.93 us
    pallas_call x1, Pallas kernels, per_device(): pl.pallas_call(functools.partial(inverse_kernel, n_row, half), out_shape=...  2.52 us
    pallas_call x1, Pallas kernels, per_device(): pl.pallas_call(functools.partial(update_kernel, n_col, False), out_shape=...  2.49 us
    pallas_call x1, Pallas kernels, per_device(): pl.pallas_call(load_kernel, out_shape=[jax.ShapeDtypeStruct(a.shape, a.dt...  0.94 us
    pallas_call x1, Pallas kernels, per_device(): pl.pallas_call(functools.partial(update_kernel, n_col, True), out_shape=[...  0.92 us
  transfers between devices with their start and end apart: 10, of which 4 were waited for; matrix products, arithmetic and copies ran while one was open for 0% of the time, Pallas kernels for 14%

profile of v6, /device:TPU:0, one launch (start us, length us, event | category | flops | bytes accessed | tf_op | source)
XLA Modules:
  0.0 31.2 jit_solution(9834222241755660604)
XLA Ops:
  0.6 0.6 %collective-permute-start.1 = (bf16[512,128]{1,0:T(8,128)(2,1)}, bf16[512,128]{1,0:T(8,128)(2,1)S(1)}, u32[]{:S(2)}, u32[]{:S(2)}) collective-permute-start(bf16[512,128]{1,0:T(8,128)(2,1)} %refs_1_.1), channel_id=1, source_target_pairs={{0,4},{4,0},{8,12},{12,8},{16,20},{20,16},{24,28},{28,24},{1,5},{5... | collective-permute-start | bytes 393224 | tf_op jit(solution)/shard_map/ppermute | solution.py:19
  1.2 0.1 collective-permute-start
  1.3 0.9 %load.1 = (f32[16,128]{1,0:T(8,128)S(1)}, bf16[512,128]{1,0:T(8,128)(2,1)S(1)}) custom-call(f32[16,128]{1,0:T(8,128)} %refs_0_.2, bf16[512,128]{1,0:T(8,128)(2,1)} %refs_1_.1), custom_call_target="tpu_custom_call" | custom-call | flops 1 | bytes 262144 | tf_op jit(solution)/shard_map/load/pallas_call | solution.py:265
  2.2 0.4 %collective-permute-done.refs_1_ = f32[16,128]{1,0:T(8,128)S(1)} collective-permute-done((f32[16,128]{1,0:T(8,128)}, f32[16,128]{1,0:T(8,128)S(1)}, u32[]{:S(2)}, u32[]{:S(2)}) %collective-permute-start) | collective-permute-done | bytes 8224 | tf_op jit(solution)/shard_map/ppermute | solution.py:19
  2.6 0.0 collective-permute-done.1.refs_3_
  2.6 3.8 %collective-permute-start.3 = (bf16[352,128]{1,0:T(8,128)(2,1)S(1)}, bf16[352,128]{1,0:T(8,128)(2,1)S(1)}, u32[]{:S(2)}, u32[]{:S(2)}) collective-permute-start(bf16[352,128]{1,0:T(8,128)(2,1)S(1)} %get-tuple-element.15), channel_id=1, source_target_pairs={{0,16},{4,20},{8,24},{12,28},{16,0},{20,4},{24,8},{28,12},{1,17},{... | collective-permute-start | bytes 270344 | tf_op jit(solution)/shard_map/ppermute | solution.py:19
  6.4 5.0 %collective-permute-done.3.refs_3_ = bf16[352,128]{1,0:T(8,128)(2,1)S(1)} collective-permute-done((bf16[352,128]{1,0:T(8,128)(2,1)S(1)}, bf16[352,128]{1,0:T(8,128)(2,1)S(1)}, u32[]{:S(2)}, u32[]{:S(2)}) %collective-permute-start.3) | collective-permute-done | bytes 90144 | tf_op jit(solution)/shard_map/ppermute | solution.py:19
  11.5 0.8 %collective-permute-start.5 = (bf16[256,128]{1,0:T(8,128)(2,1)S(1)}, bf16[256,128]{1,0:T(8,128)(2,1)S(1)}, u32[]{:S(2)}, u32[]{:S(2)}) collective-permute-start(bf16[256,128]{1,0:T(8,128)(2,1)S(1)} %slice_select_fusion), channel_id=1, source_target_pairs={{0,8},{4,12},{8,0},{12,4},{16,24},{20,28},{24,16},{28,20},{1,9},{5... | collective-permute-start | bytes 196616 | tf_op jit(solution)/shard_map/ppermute | solution.py:19
  12.3 1.5 %collective-permute-start.6 = (bf16[512,128]{1,0:T(8,128)(2,1)S(1)}, bf16[512,128]{1,0:T(8,128)(2,1)S(1)}, u32[]{:S(2)}, u32[]{:S(2)}) collective-permute-start(bf16[512,128]{1,0:T(8,128)(2,1)S(1)} %get-tuple-element.13.refs_2_.refs_3_), channel_id=1, source_target_pairs={{0,1},{1,0},{2,3},{3,2},{4,5},{5,4},{6,7},{7,6},{8,9},{9,8},{10,11... | collective-permute-start | bytes 393224 | tf_op jit(solution)/shard_map/ppermute | solution.py:19
  13.8 1.5 %collective-permute-start.8 = (bf16[512,128]{1,0:T(8,128)(2,1)S(1)}, bf16[512,128]{1,0:T(8,128)(2,1)S(1)}, u32[]{:S(2)}, u32[]{:S(2)}) collective-permute-start(bf16[512,128]{1,0:T(8,128)(2,1)S(1)} %get-tuple-element.13.refs_2_.refs_3_), channel_id=1, source_target_pairs={{0,2},{1,3},{2,0},{3,1},{4,6},{5,7},{6,4},{7,5},{8,10},{9,11},{10,... | collective-permute-start | bytes 393224 | tf_op jit(solution)/shard_map/ppermute | solution.py:19
  15.3 0.5 %collective-permute-start.9 = (bf16[512,128]{1,0:T(8,128)(2,1)S(1)}, bf16[512,128]{1,0:T(8,128)(2,1)S(1)}, u32[]{:S(2)}, u32[]{:S(2)}) collective-permute-start(bf16[512,128]{1,0:T(8,128)(2,1)S(1)} %get-tuple-element.13.refs_2_.refs_3_), channel_id=1, source_target_pairs={{0,3},{1,2},{2,1},{3,0},{4,7},{5,6},{6,5},{7,4},{8,11},{9,10},{10,... | collective-permute-start | bytes 393224 | tf_op jit(solution)/shard_map/ppermute | solution.py:19
  15.8 0.0 collective-permute-done.5
  15.8 0.1 collective-permute-start.7
  15.9 1.3 %collective-permute-start.2 = (f32[32,128]{1,0:T(8,128)S(1)}, f32[32,128]{1,0:T(8,128)S(1)}, u32[]{:S(2)}, u32[]{:S(2)}) collective-permute-start(f32[32,128]{1,0:T(8,128)S(1)} %get-tuple-element.14.refs_1_), channel_id=1, source_target_pairs={{0,8},{4,12},{8,0},{12,4},{16,24},{20,28},{24,16},{28,20},{1,9},{5... | collective-permute-start | bytes 49160 | tf_op jit(solution)/shard_map/ppermute | solution.py:19
  17.2 2.5 %collective-permute-done.2.refs_2_ = f32[32,128]{1,0:T(8,128)S(1)} collective-permute-done((f32[32,128]{1,0:T(8,128)S(1)}, f32[32,128]{1,0:T(8,128)S(1)}, u32[]{:S(2)}, u32[]{:S(2)}) %collective-permute-start.2) | collective-permute-done | bytes 16416 | tf_op jit(solution)/shard_map/ppermute | solution.py:19
  19.7 3.5 %collective-permute-start.4 = (f32[32,128]{1,0:T(8,128)S(1)}, f32[32,128]{1,0:T(8,128)S(1)}, u32[]{:S(2)}, u32[]{:S(2)}) collective-permute-start(f32[32,128]{1,0:T(8,128)S(1)} %get-tuple-element.14.refs_1_), channel_id=1, source_target_pairs={{0,24},{4,28},{8,16},{12,20},{16,8},{20,12},{24,0},{28,4},{1,25},{... | collective-permute-start | bytes 49160 | tf_op jit(solution)/shard_map/ppermute | solution.py:19
  23.2 2.0 %collective-permute-done.4.refs_4_ = f32[32,128]{1,0:T(8,128)S(1)} collective-permute-done((f32[32,128]{1,0:T(8,128)S(1)}, f32[32,128]{1,0:T(8,128)S(1)}, u32[]{:S(2)}, u32[]{:S(2)}) %collective-permute-start.4) | collective-permute-done | bytes 16416 | tf_op jit(solution)/shard_map/ppermute | solution.py:19
  25.2 2.5 %inverse.1 = (bf16[128,128]{1,0:T(8,128)(2,1)S(1)}, f32[2048,512]{1,0:T(8,128)S(1)}) custom-call(f32[2048,512]{1,0:T(8,128)} %refs_0_.3, f32[32,128]{1,0:T(8,128)S(1)} %get-tuple-element.14.refs_1_, f32[32,128]{1,0:T(8,128)S(1)} %collective-permute-done.2.refs_2_, bf16[352,128]{1,0:T(8,128)(2,1)S(1)} %collective-permute-done.3.refs_3_, ...), custom_call_target="tpu_custom_call" | custom-call | flops 4194304 | bytes 98304 | tf_op jit(solution)/shard_map/inverse/pallas_call | solution.py:311
  27.8 0.0 collective-permute-done.6.refs_4_
  27.8 0.9 %update_first.1 = (bf16[512,128]{1,0:T(8,128)(2,1)}, bf16[1024,128]{1,0:T(8,128)(2,1)S(1)}, bf16[128,256]{1,0:T(8,128)(2,1)S(1)}, f32[1024,256]{1,0:T(8,128)S(1)}) custom-call(bf16[128,128]{1,0:T(8,128)(2,1)S(1)} %get-tuple-element.16.refs_0_, bf16[256,128]{1,0:T(8,128)(2,1)S(1)} %broadcast_select_fusion.refs_1_, f32[2048,512]{1,0:T(8,128)S(1)} %get-tuple-element.17.refs_2_, ...), custom_call_target="tpu_custom_call" | custom-call | flops 134217728 | bytes 4194304 | tf_op jit(solution)/shard_map/update_first/pallas_call | solution.py:345
  28.7 0.0 collective-permute-done.8.refs_3_
  28.7 0.0 collective-permute-done.9.refs_4_
  28.7 0.0 collective-permute-done.7.refs_1_
  28.7 2.5 %update_second.1 = f32[2048,512]{1,0:T(8,128)} custom-call(bf16[128,128]{1,0:T(8,128)(2,1)S(1)} %get-tuple-element.16.refs_0_, bf16[256,128]{1,0:T(8,128)(2,1)S(1)} %collective-permute-done.7.refs_1_, f32[2048,512]{1,0:T(8,128)S(1)} %get-tuple-element.17.refs_2_, bf16[512,128]{1,0:T(8,128)(2,1)S(1)} %collective-permute-done.8.refs_3_, ...), custom_call_target="tpu_custom_call" | custom-call | flops 134217728 | bytes 4194304 | tf_op jit(solution)/shard_map/update_second/pallas_call | solution.py:354
  (3 shorter events, 0.0 us)
Async XLA Ops:
  0.6 1.9 %collective-permute-start.1 = (bf16[512,128]{1,0:T(8,128)(2,1)}, bf16[512,128]{1,0:T(8,128)(2,1)S(1)}, u32[]{:S(2)}, u32[]{:S(2)}) collective-permute-start(bf16[512,128]{1,0:T(8,128)(2,1)} %refs_1_.1), channel_id=1, source_target_pairs={{0,4},{4,0},{8,12},{12,8},{16,20},{20,16},{24,28},{28,24},{1,5},{5... | collective-permute-start | bytes 393224 | tf_op jit(solution)/shard_map/ppermute | solution.py:19
  1.2 1.4 %collective-permute-start = (f32[16,128]{1,0:T(8,128)}, f32[16,128]{1,0:T(8,128)S(1)}, u32[]{:S(2)}, u32[]{:S(2)}) collective-permute-start(f32[16,128]{1,0:T(8,128)} %refs_0_.2), channel_id=1, source_target_pairs={{0,4},{4,0},{8,12},{12,8},{16,20},{20,16},{24,28},{28,24},{1,5},{5... | collective-permute-start | bytes 24584 | tf_op jit(solution)/shard_map/ppermute | solution.py:19
  2.6 8.9 %collective-permute-start.3 = (bf16[352,128]{1,0:T(8,128)(2,1)S(1)}, bf16[352,128]{1,0:T(8,128)(2,1)S(1)}, u32[]{:S(2)}, u32[]{:S(2)}) collective-permute-start(bf16[352,128]{1,0:T(8,128)(2,1)S(1)} %get-tuple-element.15), channel_id=1, source_target_pairs={{0,16},{4,20},{8,24},{12,28},{16,0},{20,4},{24,8},{28,12},{1,17},{... | collective-permute-start | bytes 270344 | tf_op jit(solution)/shard_map/ppermute | solution.py:19
  11.5 4.3 %collective-permute-start.5 = (bf16[256,128]{1,0:T(8,128)(2,1)S(1)}, bf16[256,128]{1,0:T(8,128)(2,1)S(1)}, u32[]{:S(2)}, u32[]{:S(2)}) collective-permute-start(bf16[256,128]{1,0:T(8,128)(2,1)S(1)} %slice_select_fusion), channel_id=1, source_target_pairs={{0,8},{4,12},{8,0},{12,4},{16,24},{20,28},{24,16},{28,20},{1,9},{5... | collective-permute-start | bytes 196616 | tf_op jit(solution)/shard_map/ppermute | solution.py:19
  12.3 15.5 %collective-permute-start.6 = (bf16[512,128]{1,0:T(8,128)(2,1)S(1)}, bf16[512,128]{1,0:T(8,128)(2,1)S(1)}, u32[]{:S(2)}, u32[]{:S(2)}) collective-permute-start(bf16[512,128]{1,0:T(8,128)(2,1)S(1)} %get-tuple-element.13.refs_2_.refs_3_), channel_id=1, source_target_pairs={{0,1},{1,0},{2,3},{3,2},{4,5},{5,4},{6,7},{7,6},{8,9},{9,8},{10,11... | collective-permute-start | bytes 393224 | tf_op jit(solution)/shard_map/ppermute | solution.py:19
  13.8 14.9 %collective-permute-start.8 = (bf16[512,128]{1,0:T(8,128)(2,1)S(1)}, bf16[512,128]{1,0:T(8,128)(2,1)S(1)}, u32[]{:S(2)}, u32[]{:S(2)}) collective-permute-start(bf16[512,128]{1,0:T(8,128)(2,1)S(1)} %get-tuple-element.13.refs_2_.refs_3_), channel_id=1, source_target_pairs={{0,2},{1,3},{2,0},{3,1},{4,6},{5,7},{6,4},{7,5},{8,10},{9,11},{10,... | collective-permute-start | bytes 393224 | tf_op jit(solution)/shard_map/ppermute | solution.py:19
  15.3 13.4 %collective-permute-start.9 = (bf16[512,128]{1,0:T(8,128)(2,1)S(1)}, bf16[512,128]{1,0:T(8,128)(2,1)S(1)}, u32[]{:S(2)}, u32[]{:S(2)}) collective-permute-start(bf16[512,128]{1,0:T(8,128)(2,1)S(1)} %get-tuple-element.13.refs_2_.refs_3_), channel_id=1, source_target_pairs={{0,3},{1,2},{2,1},{3,0},{4,7},{5,6},{6,5},{7,4},{8,11},{9,10},{10,... | collective-permute-start | bytes 393224 | tf_op jit(solution)/shard_map/ppermute | solution.py:19
  15.8 12.9 %collective-permute-start.7 = (bf16[256,128]{1,0:T(8,128)(2,1)S(1)}, bf16[256,128]{1,0:T(8,128)(2,1)S(1)}, u32[]{:S(2)}, u32[]{:S(2)}) collective-permute-start(bf16[256,128]{1,0:T(8,128)(2,1)S(1)} %broadcast_select_fusion.refs_1_), channel_id=1, source_target_pairs={{0,4},{4,0},{8,12},{12,8},{16,20},{20,16},{24,28},{28,24},{1,5},{5... | collective-permute-start | bytes 196616 | tf_op jit(solution)/shard_map/ppermute | solution.py:19
  15.9 3.8 %collective-permute-start.2 = (f32[32,128]{1,0:T(8,128)S(1)}, f32[32,128]{1,0:T(8,128)S(1)}, u32[]{:S(2)}, u32[]{:S(2)}) collective-permute-start(f32[32,128]{1,0:T(8,128)S(1)} %get-tuple-element.14.refs_1_), channel_id=1, source_target_pairs={{0,8},{4,12},{8,0},{12,4},{16,24},{20,28},{24,16},{28,20},{1,9},{5... | collective-permute-start | bytes 49160 | tf_op jit(solution)/shard_map/ppermute | solution.py:19
  19.7 5.5 %collective-permute-start.4 = (f32[32,128]{1,0:T(8,128)S(1)}, f32[32,128]{1,0:T(8,128)S(1)}, u32[]{:S(2)}, u32[]{:S(2)}) collective-permute-start(f32[32,128]{1,0:T(8,128)S(1)} %get-tuple-element.14.refs_1_), channel_id=1, source_target_pairs={{0,24},{4,28},{8,16},{12,20},{16,8},{20,12},{24,0},{28,4},{1,25},{... | collective-permute-start | bytes 49160 | tf_op jit(solution)/shard_map/ppermute | solution.py:19

commit v7 on v6

--- a/solution.py
+++ b/solution.py
@@ -44,11 +44,13 @@
     )
 
 
-def tree_steps(n_row):
-    steps = [n_row // 4]
-    while steps[-1] > 2:
-        steps.append(steps[-1] // 2)
-    return steps
+def paired_steps(n_row):
+    return len(far_steps(n_row)) == 3
+
+
+def exchange_far(value, n_row):
+    pairs = [(i, i ^ (n_row - 2 if i % 2 else n_row // 2)) for i in range(n_row)]
+    return lax.ppermute(value, "row", pairs)
 
 
 def inverse_factor(tile):
@@ -137,23 +139,25 @@
                 pack[start : start + depth, :] = value.astype(jnp.bfloat16)
 
 
-def inverse_kernel(n_row, half, *refs):
+def inverse_kernel(steps, *refs):
     trailing, *packs, out, held, tile, sem = refs
     load = pltpu.make_async_copy(trailing, held, sem)
     load.start()
     me = lax.axis_index("row")
-    depth = tile.shape[0] // n_row
-    for step, pack in zip(range(0, n_row, 2), packs):
+    odd = lax.rem(me, 2)
+    depth = packs[0].shape[0] // 2
+    for (step, turn, crossed), pack in zip(steps, packs):
+        step = step + odd * turn
         for i in range(2):
             if pack.dtype == tile.dtype:
                 value = pack[i * depth : (i + 1) * depth, :]
             else:
                 parts = []
                 for term in range(3):
-                    start = half + (2 * term + i) * depth
+                    start = pack.shape[0] - (6 - 2 * term - i) * depth
                     parts.append(pack[start : start + depth, :].astype(jnp.float32))
                 value = (parts[0] + parts[1]) + parts[2]
-            place = pl.multiple_of((me ^ step ^ i) * depth, depth)
+            place = pl.multiple_of((me ^ step ^ (i ^ crossed)) * depth, depth)
             tile[pl.ds(place, depth), :] = value
 
     @pl.when(me >= 0)
@@ -260,7 +264,7 @@
 def per_device(n_row, n_col, diag_tile, panel, trailing):
     rows_dev, cols_dev = trailing.shape
     depth, width = panel.shape
-    direct = depth == cols_dev and n_col * cols_dev <= rows_dev
+    direct = depth == cols_dev and n_col * cols_dev <= rows_dev and paired_steps(n_row)
     half = depth // 2 if direct else 0
     tile_near, panel_near = pl.pallas_call(
         load_kernel,
@@ -293,28 +297,33 @@
         compiler_params=pltpu.CompilerParams(vmem_limit_bytes=4 * 1024 * 1024),
         name="pack",
     )(*packed)
-    middle = n_row // 2
-    packs = {0: two}
-    for step in far_steps(n_row):
-        value = pack[0] if direct and step == middle else two
-        packs[step] = exchange(value, "row", n_row, step)
     row = lax.axis_index("row")
+    odd = row % 2 == 1
+    packs, steps = [two], [(0, 0, 0)]
     if direct:
-        near = jnp.where(row & middle != 0, packs[middle][:half], pack[0][:half])
-        for step in tree_steps(n_row):
-            came = exchange(near, "row", n_row, step)
-            near = jnp.where(row & step != 0, came, near)
+        middle, last = n_row // 2, n_row - 2
+        came = exchange_far(pack[0], n_row)
+        packs.append(exchange(two, "row", n_row, 2))
+        packs += [came, exchange(came[half:], "row", n_row, 1)]
+        steps += [(2, 0, 0), (middle, last - middle, 0), (last, middle - last, 1)]
+        chip = row & ~1
+        reached = jnp.where(odd, last, middle)
+        near = jnp.where(chip == reached, came[:half], pack[0][:half])
+        came = exchange(near, "row", n_row, 2)
+        near = jnp.where((chip == 2) | (chip == (reached ^ 2)), came, near)
         other = exchange(near, "row", n_row, 1)
     else:
+        for step in far_steps(n_row):
+            packs.append(exchange(two, "row", n_row, step))
+            steps.append((step, 0, 0))
         near, other = column_rows(panel, n_col, cols_dev)
-    packs = [packs[step] for step in range(0, n_row, 2)]
     inverse, held = pl.pallas_call(
-        functools.partial(inverse_kernel, n_row, half),
+        functools.partial(inverse_kernel, steps),
         out_shape=[
             jax.ShapeDtypeStruct((width, width), jnp.bfloat16),
             jax.ShapeDtypeStruct(trailing.shape, trailing.dtype),
         ],
-        in_specs=[HBM] + [VMEM] * (n_row // 2),
+        in_specs=[HBM] + [VMEM] * len(packs),
         out_specs=[VMEM] * 2,
         scratch_shapes=[
             pltpu.VMEM((width, width), jnp.float32),

time: 31.5 us -> 27.3 us (0.87)
  starting transfers between devices: 13.7 us -> 9.64 us
    ppermute x10 -> x9, starting transfers between devices: 13.7 us -> 5.82 us  [exchange(): return lax.ppermute(value, axis, [(i, i ^ step) for i in range(size)])]
    ppermute x10 -> x9, waiting for transfers between devices: 9.93 us -> 4.59 us  [exchange(): return lax.ppermute(value, axis, [(i, i ^ step) for i in range(size)])]
    ppermute x0 -> x1, waiting for transfers between devices: none -> 5.2 us  [exchange_far(): return lax.ppermute(value, 'row', pairs)]
    ppermute x0 -> x1, starting transfers between devices: none -> 3.82 us  [exchange_far(): return lax.ppermute(value, 'row', pairs)]
  transfers between devices with their start and end apart: 10 -> 10, of which waited for: 4 -> 5; matrix products, arithmetic and copies ran while one was open for 0% -> 0% of each run, Pallas kernels for 14% -> 16%
where the time goes in v7:
time: 27.3 us; the launch traced here: 27.1 us
  waiting for transfers between devices  9.79 us (36%)
  starting transfers between devices  9.64 us (35%)
  Pallas kernels  6.89 us (25%)
  between operations  0.71 us (3%)
    ppermute x9, starting transfers between devices, exchange(): return lax.ppermute(value, axis, [(i, i ^ step) for i in range(size)])  5.82 us
    ppermute x1, waiting for transfers between devices, exchange_far(): return lax.ppermute(value, 'row', pairs)  5.2 us
    ppermute x9, waiting for transfers between devices, exchange(): return lax.ppermute(value, axis, [(i, i ^ step) for i in range(size)])  4.59 us
    ppermute x1, starting transfers between devices, exchange_far(): return lax.ppermute(value, 'row', pairs)  3.82 us
    pallas_call x1, Pallas kernels, per_device(): pl.pallas_call(functools.partial(inverse_kernel, steps), out_shape=[jax.S...  2.53 us
    pallas_call x1, Pallas kernels, per_device(): pl.pallas_call(functools.partial(update_kernel, n_col, False), out_shape=...  2.49 us
    pallas_call x1, Pallas kernels, per_device(): pl.pallas_call(load_kernel, out_shape=[jax.ShapeDtypeStruct(a.shape, a.dt...  0.94 us
    pallas_call x1, Pallas kernels, per_device(): pl.pallas_call(functools.partial(update_kernel, n_col, True), out_shape=[...  0.91 us
  transfers between devices with their start and end apart: 10, of which 5 were waited for; matrix products, arithmetic and copies ran while one was open for 0% of the time, Pallas kernels for 16%

profile of v7, /device:TPU:0, one launch (start us, length us, event | category | flops | bytes accessed | tf_op | source)
XLA Modules:
  0.0 27.1 jit_solution(18199033173435823565)
XLA Ops:
  0.6 0.6 %collective-permute-start.1 = (bf16[512,128]{1,0:T(8,128)(2,1)}, bf16[512,128]{1,0:T(8,128)(2,1)S(1)}, u32[]{:S(2)}, u32[]{:S(2)}) collective-permute-start(bf16[512,128]{1,0:T(8,128)(2,1)} %refs_1_.1), channel_id=1, source_target_pairs={{0,4},{4,0},{8,12},{12,8},{16,20},{20,16},{24,28},{28,24},{1,5},{5... | collective-permute-start | bytes 393224 | tf_op jit(solution)/shard_map/ppermute | solution.py:19
  1.2 0.1 collective-permute-start
  1.3 0.9 %load.1 = (f32[16,128]{1,0:T(8,128)S(1)}, bf16[512,128]{1,0:T(8,128)(2,1)S(1)}) custom-call(f32[16,128]{1,0:T(8,128)} %refs_0_.2, bf16[512,128]{1,0:T(8,128)(2,1)} %refs_1_.1), custom_call_target="tpu_custom_call" | custom-call | flops 1 | bytes 262144 | tf_op jit(solution)/shard_map/load/pallas_call | solution.py:269
  2.2 0.4 %collective-permute-done.refs_1_ = f32[16,128]{1,0:T(8,128)S(1)} collective-permute-done((f32[16,128]{1,0:T(8,128)}, f32[16,128]{1,0:T(8,128)S(1)}, u32[]{:S(2)}, u32[]{:S(2)}) %collective-permute-start) | collective-permute-done | bytes 8224 | tf_op jit(solution)/shard_map/ppermute | solution.py:19
  2.6 0.0 collective-permute-done.1.refs_3_
  2.6 3.8 %collective-permute-start.3 = (bf16[352,128]{1,0:T(8,128)(2,1)S(1)}, bf16[352,128]{1,0:T(8,128)(2,1)S(1)}, u32[]{:S(2)}, u32[]{:S(2)}) collective-permute-start(bf16[352,128]{1,0:T(8,128)(2,1)S(1)} %get-tuple-element.15), channel_id=1, source_target_pairs={{0,16},{4,28},{8,24},{12,20},{16,0},{20,12},{24,8},{28,4},{1,17},{... | collective-permute-start | bytes 270344 | tf_op jit(solution)/shard_map/ppermute | solution.py:53
  6.4 5.2 %collective-permute-done.3.refs_3_ = bf16[352,128]{1,0:T(8,128)(2,1)S(1)} collective-permute-done((bf16[352,128]{1,0:T(8,128)(2,1)S(1)}, bf16[352,128]{1,0:T(8,128)(2,1)S(1)}, u32[]{:S(2)}, u32[]{:S(2)}) %collective-permute-start.3) | collective-permute-done | bytes 90144 | tf_op jit(solution)/shard_map/ppermute | solution.py:53
  11.6 0.3 %collective-permute-start.5 = (bf16[256,128]{1,0:T(8,128)(2,1)S(1)}, bf16[256,128]{1,0:T(8,128)(2,1)S(1)}, u32[]{:S(2)}, u32[]{:S(2)}) collective-permute-start(bf16[256,128]{1,0:T(8,128)(2,1)S(1)} %slice_select_fusion), channel_id=1, source_target_pairs={{0,8},{4,12},{8,0},{12,4},{16,24},{20,28},{24,16},{28,20},{1,9},{5... | collective-permute-start | bytes 196616 | tf_op jit(solution)/shard_map/ppermute | solution.py:19
  11.9 1.5 %collective-permute-start.6 = (bf16[512,128]{1,0:T(8,128)(2,1)S(1)}, bf16[512,128]{1,0:T(8,128)(2,1)S(1)}, u32[]{:S(2)}, u32[]{:S(2)}) collective-permute-start(bf16[512,128]{1,0:T(8,128)(2,1)S(1)} %get-tuple-element.13.refs_2_.refs_3_), channel_id=1, source_target_pairs={{0,1},{1,0},{2,3},{3,2},{4,5},{5,4},{6,7},{7,6},{8,9},{9,8},{10,11... | collective-permute-start | bytes 393224 | tf_op jit(solution)/shard_map/ppermute | solution.py:19
  13.4 1.5 %collective-permute-start.8 = (bf16[512,128]{1,0:T(8,128)(2,1)S(1)}, bf16[512,128]{1,0:T(8,128)(2,1)S(1)}, u32[]{:S(2)}, u32[]{:S(2)}) collective-permute-start(bf16[512,128]{1,0:T(8,128)(2,1)S(1)} %get-tuple-element.13.refs_2_.refs_3_), channel_id=1, source_target_pairs={{0,2},{1,3},{2,0},{3,1},{4,6},{5,7},{6,4},{7,5},{8,10},{9,11},{10,... | collective-permute-start | bytes 393224 | tf_op jit(solution)/shard_map/ppermute | solution.py:19
  15.0 0.5 %collective-permute-start.9 = (bf16[512,128]{1,0:T(8,128)(2,1)S(1)}, bf16[512,128]{1,0:T(8,128)(2,1)S(1)}, u32[]{:S(2)}, u32[]{:S(2)}) collective-permute-start(bf16[512,128]{1,0:T(8,128)(2,1)S(1)} %get-tuple-element.13.refs_2_.refs_3_), channel_id=1, source_target_pairs={{0,3},{1,2},{2,1},{3,0},{4,7},{5,6},{6,5},{7,4},{8,11},{9,10},{10,... | collective-permute-start | bytes 393224 | tf_op jit(solution)/shard_map/ppermute | solution.py:19
  15.4 0.5 %collective-permute-done.5 = bf16[256,128]{1,0:T(8,128)(2,1)S(1)} collective-permute-done((bf16[256,128]{1,0:T(8,128)(2,1)S(1)}, bf16[256,128]{1,0:T(8,128)(2,1)S(1)}, u32[]{:S(2)}, u32[]{:S(2)}) %collective-permute-start.5) | collective-permute-done | bytes 65568 | tf_op jit(solution)/shard_map/ppermute | solution.py:19
  16.0 0.1 collective-permute-start.7
  16.1 1.3 %collective-permute-start.2 = (f32[32,128]{1,0:T(8,128)S(1)}, f32[32,128]{1,0:T(8,128)S(1)}, u32[]{:S(2)}, u32[]{:S(2)}) collective-permute-start(f32[32,128]{1,0:T(8,128)S(1)} %get-tuple-element.14.refs_1_), channel_id=1, source_target_pairs={{0,8},{4,12},{8,0},{12,4},{16,24},{20,28},{24,16},{28,20},{1,9},{5... | collective-permute-start | bytes 49160 | tf_op jit(solution)/shard_map/ppermute | solution.py:19
  17.4 2.5 %collective-permute-done.2.refs_2_ = f32[32,128]{1,0:T(8,128)S(1)} collective-permute-done((f32[32,128]{1,0:T(8,128)S(1)}, f32[32,128]{1,0:T(8,128)S(1)}, u32[]{:S(2)}, u32[]{:S(2)}) %collective-permute-start.2) | collective-permute-done | bytes 16416 | tf_op jit(solution)/shard_map/ppermute | solution.py:19
  19.9 0.0 collective-permute-start.4
  19.9 1.2 %collective-permute-done.4.refs_4_ = bf16[96,128]{1,0:T(8,128)(2,1)S(1)} collective-permute-done((bf16[96,128]{1,0:T(8,128)(2,1)S(1)}, bf16[96,128]{1,0:T(8,128)(2,1)S(1)}, u32[]{:S(2)}, u32[]{:S(2)}) %collective-permute-start.4) | collective-permute-done | bytes 24608 | tf_op jit(solution)/shard_map/ppermute | solution.py:19
  21.1 2.5 %inverse.1 = (bf16[128,128]{1,0:T(8,128)(2,1)S(1)}, f32[2048,512]{1,0:T(8,128)S(1)}) custom-call(f32[2048,512]{1,0:T(8,128)} %refs_0_.3, f32[32,128]{1,0:T(8,128)S(1)} %get-tuple-element.14.refs_1_, f32[32,128]{1,0:T(8,128)S(1)} %collective-permute-done.2.refs_2_, bf16[352,128]{1,0:T(8,128)(2,1)S(1)} %collective-permute-done.3.refs_3_, ...), custom_call_target="tpu_custom_call" | custom-call | flops 4194304 | bytes 98304 | tf_op jit(solution)/shard_map/inverse/pallas_call | solution.py:320
  23.6 0.0 collective-permute-done.6.refs_4_
  23.6 0.9 %update_first.1 = (bf16[512,128]{1,0:T(8,128)(2,1)}, bf16[1024,128]{1,0:T(8,128)(2,1)S(1)}, bf16[128,256]{1,0:T(8,128)(2,1)S(1)}, f32[1024,256]{1,0:T(8,128)S(1)}) custom-call(bf16[128,128]{1,0:T(8,128)(2,1)S(1)} %get-tuple-element.16.refs_0_, bf16[256,128]{1,0:T(8,128)(2,1)S(1)} %broadcast_select_fusion.refs_1_, f32[2048,512]{1,0:T(8,128)S(1)} %get-tuple-element.17.refs_2_, ...), custom_call_target="tpu_custom_call" | custom-call | flops 134217728 | bytes 4194304 | tf_op jit(solution)/shard_map/update_first/pallas_call | solution.py:354
  24.5 0.0 collective-permute-done.8.refs_3_
  24.5 0.0 collective-permute-done.9.refs_4_
  24.6 0.0 collective-permute-done.7.refs_1_
  24.6 2.5 %update_second.1 = f32[2048,512]{1,0:T(8,128)} custom-call(bf16[128,128]{1,0:T(8,128)(2,1)S(1)} %get-tuple-element.16.refs_0_, bf16[256,128]{1,0:T(8,128)(2,1)S(1)} %collective-permute-done.7.refs_1_, f32[2048,512]{1,0:T(8,128)S(1)} %get-tuple-element.17.refs_2_, bf16[512,128]{1,0:T(8,128)(2,1)S(1)} %collective-permute-done.8.refs_3_, ...), custom_call_target="tpu_custom_call" | custom-call | flops 134217728 | bytes 4194304 | tf_op jit(solution)/shard_map/update_second/pallas_call | solution.py:363
  (4 shorter events, 0.0 us)
Async XLA Ops:
  0.6 1.9 %collective-permute-start.1 = (bf16[512,128]{1,0:T(8,128)(2,1)}, bf16[512,128]{1,0:T(8,128)(2,1)S(1)}, u32[]{:S(2)}, u32[]{:S(2)}) collective-permute-start(bf16[512,128]{1,0:T(8,128)(2,1)} %refs_1_.1), channel_id=1, source_target_pairs={{0,4},{4,0},{8,12},{12,8},{16,20},{20,16},{24,28},{28,24},{1,5},{5... | collective-permute-start | bytes 393224 | tf_op jit(solution)/shard_map/ppermute | solution.py:19
  1.2 1.4 %collective-permute-start = (f32[16,128]{1,0:T(8,128)}, f32[16,128]{1,0:T(8,128)S(1)}, u32[]{:S(2)}, u32[]{:S(2)}) collective-permute-start(f32[16,128]{1,0:T(8,128)} %refs_0_.2), channel_id=1, source_target_pairs={{0,4},{4,0},{8,12},{12,8},{16,20},{20,16},{24,28},{28,24},{1,5},{5... | collective-permute-start | bytes 24584 | tf_op jit(solution)/shard_map/ppermute | solution.py:19
  2.6 9.0 %collective-permute-start.3 = (bf16[352,128]{1,0:T(8,128)(2,1)S(1)}, bf16[352,128]{1,0:T(8,128)(2,1)S(1)}, u32[]{:S(2)}, u32[]{:S(2)}) collective-permute-start(bf16[352,128]{1,0:T(8,128)(2,1)S(1)} %get-tuple-element.15), channel_id=1, source_target_pairs={{0,16},{4,28},{8,24},{12,20},{16,0},{20,12},{24,8},{28,4},{1,17},{... | collective-permute-start | bytes 270344 | tf_op jit(solution)/shard_map/ppermute | solution.py:53
  11.6 4.3 %collective-permute-start.5 = (bf16[256,128]{1,0:T(8,128)(2,1)S(1)}, bf16[256,128]{1,0:T(8,128)(2,1)S(1)}, u32[]{:S(2)}, u32[]{:S(2)}) collective-permute-start(bf16[256,128]{1,0:T(8,128)(2,1)S(1)} %slice_select_fusion), channel_id=1, source_target_pairs={{0,8},{4,12},{8,0},{12,4},{16,24},{20,28},{24,16},{28,20},{1,9},{5... | collective-permute-start | bytes 196616 | tf_op jit(solution)/shard_map/ppermute | solution.py:19
  11.9 11.7 %collective-permute-start.6 = (bf16[512,128]{1,0:T(8,128)(2,1)S(1)}, bf16[512,128]{1,0:T(8,128)(2,1)S(1)}, u32[]{:S(2)}, u32[]{:S(2)}) collective-permute-start(bf16[512,128]{1,0:T(8,128)(2,1)S(1)} %get-tuple-element.13.refs_2_.refs_3_), channel_id=1, source_target_pairs={{0,1},{1,0},{2,3},{3,2},{4,5},{5,4},{6,7},{7,6},{8,9},{9,8},{10,11... | collective-permute-start | bytes 393224 | tf_op jit(solution)/shard_map/ppermute | solution.py:19
  13.4 11.1 %collective-permute-start.8 = (bf16[512,128]{1,0:T(8,128)(2,1)S(1)}, bf16[512,128]{1,0:T(8,128)(2,1)S(1)}, u32[]{:S(2)}, u32[]{:S(2)}) collective-permute-start(bf16[512,128]{1,0:T(8,128)(2,1)S(1)} %get-tuple-element.13.refs_2_.refs_3_), channel_id=1, source_target_pairs={{0,2},{1,3},{2,0},{3,1},{4,6},{5,7},{6,4},{7,5},{8,10},{9,11},{10,... | collective-permute-start | bytes 393224 | tf_op jit(solution)/shard_map/ppermute | solution.py:19
  15.0 9.6 %collective-permute-start.9 = (bf16[512,128]{1,0:T(8,128)(2,1)S(1)}, bf16[512,128]{1,0:T(8,128)(2,1)S(1)}, u32[]{:S(2)}, u32[]{:S(2)}) collective-permute-start(bf16[512,128]{1,0:T(8,128)(2,1)S(1)} %get-tuple-element.13.refs_2_.refs_3_), channel_id=1, source_target_pairs={{0,3},{1,2},{2,1},{3,0},{4,7},{5,6},{6,5},{7,4},{8,11},{9,10},{10,... | collective-permute-start | bytes 393224 | tf_op jit(solution)/shard_map/ppermute | solution.py:19
  16.0 8.6 %collective-permute-start.7 = (bf16[256,128]{1,0:T(8,128)(2,1)S(1)}, bf16[256,128]{1,0:T(8,128)(2,1)S(1)}, u32[]{:S(2)}, u32[]{:S(2)}) collective-permute-start(bf16[256,128]{1,0:T(8,128)(2,1)S(1)} %broadcast_select_fusion.refs_1_), channel_id=1, source_target_pairs={{0,4},{4,0},{8,12},{12,8},{16,20},{20,16},{24,28},{28,24},{1,5},{5... | collective-permute-start | bytes 196616 | tf_op jit(solution)/shard_map/ppermute | solution.py:19
  16.1 3.8 %collective-permute-start.2 = (f32[32,128]{1,0:T(8,128)S(1)}, f32[32,128]{1,0:T(8,128)S(1)}, u32[]{:S(2)}, u32[]{:S(2)}) collective-permute-start(f32[32,128]{1,0:T(8,128)S(1)} %get-tuple-element.14.refs_1_), channel_id=1, source_target_pairs={{0,8},{4,12},{8,0},{12,4},{16,24},{20,28},{24,16},{28,20},{1,9},{5... | collective-permute-start | bytes 49160 | tf_op jit(solution)/shard_map/ppermute | solution.py:19
  19.9 1.2 %collective-permute-start.4 = (bf16[96,128]{1,0:T(8,128)(2,1)S(1)}, bf16[96,128]{1,0:T(8,128)(2,1)S(1)}, u32[]{:S(2)}, u32[]{:S(2)}) collective-permute-start(bf16[96,128]{1,0:T(8,128)(2,1)S(1)} %slice.12), channel_id=1, source_target_pairs={{0,4},{4,0},{8,12},{12,8},{16,20},{20,16},{24,28},{28,24},{1,5},{5... | collective-permute-start | bytes 73736 | tf_op jit(solution)/shard_map/ppermute | solution.py:19
